TPU v7x, 32 devices: a whole 2x2x4 slice. The times are simulated.
32 devices in a mesh: wa: 4 (over z), ha: 8 (over y, x, core).
Axes of the slice: x: 2, y: 2, z: 4, core: 2. Of those that a mesh axis runs over, the one named last changes fastest.
Arguments:
- tokens: bfloat16 [1024, 16384], P('ha', 'wa'), may hold values from -6 to 6
- gain_attn: bfloat16 [16384], P('wa'), may hold values from 0.25 to 1.75
- w_query: bfloat16 [16384, 16384], P('wa', 'ha'), may hold values from -0.046875 to 0.046875, as said below
- w_key: bfloat16 [16384, 1024], P('wa'), may hold values from -1.171875 to 1.171875, as said below
- w_value: bfloat16 [16384, 1024], P('wa'), may hold values from -0.046875 to 0.046875
- w_out: bfloat16 [16384, 16384], P('ha', 'wa'), may hold values from -0.1875 to 0.1875
- gain_ffn: bfloat16 [16384], P('wa'), may hold values from 0.25 to 1.75
- segment_ids: int32 [1024], replicated, may hold values from 0 to 31, never falling along the last dimension, each value on 1 to 256 neighbouring positions
Outputs:
- residual_out: bfloat16 [1024, 16384], P('ha', 'wa')
- ffn_input: bfloat16 [1024, 16384], P('ha', 'wa')
Inputs may be any that keep to these rules, and one draw needn't show every extreme that they name: `w_query`: entries scaled by 16384 ** -0.5. `w_key`: entries scaled by 16384 ** -0.5. `segment_ids`: segment ids never fall along the tokens; each prompt has 1 to 256 tokens and one has exactly 256.
All inputs are finite; a program needn't handle non-finite values.
Results may differ from a plain program's by a relative error of at most 0.00675.
The roundings to bfloat16 on the way count: a program that leaves them out, or rounds other values in their place, can miss the bound.
Values may be sent and summed in bfloat16 or wider, within the bound.
A program may use at most 192 MiB of HBM per device.

v0:
```python
import jax
import jax.numpy as jnp
from jax import lax
from jax.sharding import PartitionSpec as P

KVH = 8
HD = 128


EPS = 1e-05


def rope_tables(position):
    half = HD // 2
    inverse = 500000.0 ** (-(jnp.arange(half, dtype=jnp.float32) * 2.0 / HD))
    angle = position[:, None] * inverse[None, :]
    return (jnp.cos(angle), jnp.sin(angle))


def rotate(values, cosine, sine):
    half = values.shape[-1] // 2
    first = values[..., :half]
    second = values[..., half:]
    cosine = cosine[:, None, :]
    sine = sine[:, None, :]
    return jnp.concatenate(
        [first * cosine - second * sine, second * cosine + first * sine], axis=-1
    )


def on_device(tokens, gain_attn, w_query, w_key, w_value, w_out, gain_ffn, segment_ids):
    rows_dev, width_dev = tokens.shape
    n_wa = lax.axis_size("wa")
    n_ha = lax.axis_size("ha")
    total = rows_dev * n_ha
    width = width_dev * n_wa
    head_cols = w_query.shape[1]
    heads_dev = head_cols // HD
    token_f = tokens.astype(jnp.float32)
    gain_one = gain_attn.astype(jnp.float32)
    kv_head = lax.axis_index("ha") // (n_ha // KVH)
    kv_weights = jnp.concatenate(
        [
            lax.dynamic_slice_in_dim(w_key, kv_head * HD, HD, 1),
            lax.dynamic_slice_in_dim(w_value, kv_head * HD, HD, 1),
        ],
        axis=1,
    )
    gathered = lax.all_gather(tokens, "ha", axis=0, tiled=True)
    own_sq = lax.psum(jnp.sum(token_f * token_f, axis=1), "wa")
    own_scale = lax.rsqrt(own_sq / width + EPS)
    row_scale = lax.all_gather(own_scale, "ha", axis=0, tiled=True)
    scaled = (gathered.astype(jnp.float32) * gain_one).astype(jnp.bfloat16)
    kv_part = jnp.dot(scaled, kv_weights, preferred_element_type=jnp.float32)
    kv_sum = lax.psum(kv_part, "wa")
    index_all = jnp.arange(total, dtype=jnp.int32)
    fresh = jnp.concatenate([jnp.ones((1,), dtype=bool), segment_ids[1:] != segment_ids[:-1]])
    start_all = lax.cummax(jnp.where(fresh, index_all, jnp.zeros_like(index_all)), axis=0)
    cosine, sine = rope_tables((index_all - start_all).astype(jnp.float32))
    key_plain = (kv_sum[:, :HD] * row_scale[:, None]).astype(jnp.bfloat16)
    key_plain = lax.optimization_barrier(key_plain)
    value_head = (kv_sum[:, HD:] * row_scale[:, None]).astype(jnp.bfloat16)
    key_head = rotate(key_plain.astype(jnp.float32).reshape(total, 1, HD), cosine, sine)
    key_head = key_head.reshape(total, HD).astype(jnp.bfloat16)
    q_rows = total // n_wa
    first = lax.axis_index("wa") * q_rows
    block = scaled
    query_f = lax.psum_scatter(
        jnp.dot(block, w_query, preferred_element_type=jnp.float32),
        "wa",
        scatter_dimension=0,
        tiled=True,
    )
    q_scale = lax.dynamic_slice_in_dim(row_scale, first, q_rows, 0)
    q_cos = lax.dynamic_slice_in_dim(cosine, first, q_rows, 0)
    q_sin = lax.dynamic_slice_in_dim(sine, first, q_rows, 0)
    queries = rotate(
        (query_f * q_scale[:, None]).reshape(q_rows, heads_dev, HD), q_cos, q_sin
    ).astype(jnp.bfloat16)
    q_segment = lax.dynamic_slice_in_dim(segment_ids, first, q_rows, 0)
    q_index = first + jnp.arange(q_rows, dtype=jnp.int32)
    allowed = (q_segment[:, None] == segment_ids[None, :]) & (
        index_all[None, :] <= q_index[:, None]
    )
    scores = jnp.einsum(
        "thd,sd->hts", queries, key_head, preferred_element_type=jnp.float32
    ) * HD ** (-0.5)
    scores = jnp.where(allowed[None], scores, -1e30)
    peak = jnp.max(scores, axis=-1, keepdims=True)
    expo = jnp.where(allowed[None], jnp.exp(scores - peak), 0.0)
    weights = (expo / jnp.sum(expo, axis=-1, keepdims=True)).astype(jnp.bfloat16)
    head_out = jnp.einsum("hts,sd->thd", weights, value_head, preferred_element_type=jnp.float32)
    head_out = head_out.astype(jnp.bfloat16).reshape(q_rows, head_cols)
    head_all = lax.all_gather(head_out, "wa", axis=0, tiled=True)
    block = head_all
    attended = lax.psum_scatter(
        jnp.dot(block, w_out, preferred_element_type=jnp.float32),
        "ha",
        scatter_dimension=0,
        tiled=True,
    )
    residual_out = (token_f + attended).astype(jnp.bfloat16)
    residual_f = residual_out.astype(jnp.float32)
    square_two = lax.psum(jnp.sum(residual_f * residual_f, axis=1), "wa")
    scale_two = lax.rsqrt(square_two / width + EPS)
    ffn_input = (residual_f * scale_two[:, None] * gain_ffn.astype(jnp.float32)).astype(
        jnp.bfloat16
    )
    return (residual_out, ffn_input)


def solution(mesh):
    in_specs = (
        P("ha", "wa"),
        P("wa"),
        P("wa", "ha"),
        P("wa", None),
        P("wa", None),
        P("ha", "wa"),
        P("wa"),
        P(),
    )
    out_specs = (P("ha", "wa"), P("ha", "wa"))
    return jax.shard_map(
        on_device, mesh=mesh, in_specs=in_specs, out_specs=out_specs, check_vma=False
    )
```

profile of v0, /device:TPU:0, one launch (start us, length us, event | category | flops | bytes accessed | tf_op | source)
XLA Modules:
  0.0 537.4 jit_solution(1475122119710769772)
XLA Ops:
  7.2 0.7 all-gather.4.cloned.1.call-update
  7.9 0.7 convert_element_type.54
  8.6 1.7 constant_dynamic-slice_fusion
  10.3 56.5 %all-gather.4.cloned.1.call-done = bf16[1024,4096]{1,0:T(8,128)(2,1)} async-done(((bf16[128,4096]{1,0:T(8,128)(2,1)}), bf16[1024,4096]{1,0:T(8,128)(2,1)}) %all-gather.4.cloned.1.call-update) | async-done | bytes 8388624 | tf_op jit(solution)/shard_map/all_gather | solution.py:49
  66.9 6.7 %fusion.7 = f32[1024,256]{0,1:T(8,128)} fusion(bf16[1024,4096]{1,0:T(8,128)(2,1)} %all-gather.4.cloned.1.call-done, f32[4096]{0:T(1024)S(1)} %convert_element_type.54, bf16[4096,128]{1,0:T(8,128)(2,1)S(1)} %get-tuple-element.14, bf16[4096,128]{1,0:T(8,128)(2,1)S(1)} %get-tuple-element.15), kind=kOutput, calls=%fused_computation.11 | convolution fusion | flops 2164260864 | bytes 11550720 | tf_op jit(solution)/shard_map/dot_general | solution.py:54
  73.7 24.0 %fusion.6 = f32[1024,2048]{1,0:T(8,128)} fusion(bf16[4096,2048]{1,0:T(8,128)(2,1)} %param.10, bf16[1024,4096]{1,0:T(8,128)(2,1)} %all-gather.4.cloned.1.call-done, f32[4096]{0:T(1024)S(1)} %convert_element_type.54), kind=kOutput, calls=%fused_computation.10 | convolution fusion | flops 17192452096 | bytes 33570816 | tf_op jit(solution)/shard_map/dot_general | solution.py:69
  97.8 1.1 copy-done
  99.2 11.7 %psum.22 = f32[128]{0:T(128)S(1)} all-reduce(f32[128]{0:T(128)S(1)} %fusion.8), channel_id=1, replica_groups=mesh['wa'=4,'ha'=8] {'wa'}, use_global_device_ids=true, to_apply=%region_2.3 | all-reduce | flops 128 | bytes 1024 | tf_op jit(solution)/shard_map/psum | solution.py:50
  111.0 8.9 %all-gather = f32[8,1,128]{2,1,0:T(1,128)S(1)} all-gather(f32[1,1,128]{2,1,0:T(1,128)S(1)} %rsqrt_bitcast_fusion), channel_id=1, replica_groups=mesh['wa'=4,'ha'=8] {'ha'}, dimensions={0}, use_global_device_ids=true | all-gather | bytes 4608 | tf_op jit(solution)/shard_map/all_gather | solution.py:52
  121.4 1.0 fusion.19
  122.4 3.3 all-reduce.2.cloned.1.call-done
  125.7 1.1 fusion.20
  126.8 1.8 fusion.27
  128.6 143.4 %reduce-scatter.3.cloned.1.call-done = f32[256,2048]{1,0:T(8,128)} async-done(((f32[1024,2048]{1,0:T(8,128)}), f32[256,2048]{1,0:T(8,128)}) %reduce-scatter.3.cloned.1.call-update) | async-done | bytes 2097168 | tf_op jit(solution)/shard_map/reduce_scatter | solution.py:68
  272.0 1.8 multiply_bitcast_fusion
  274.9 1.4 subtract_convert_fusion
  276.2 11.8 %fusion.44 = (f32[16,256]{1,0:T(8,128)S(1)}, f32[16,256,1024]{1,2,0:T(8,128)}) fusion(pred[256,1024]{0,1:T(8,128)(4,1)} %fusion.19, bf16[1024,1,64]{0,2,1:T(8,128)(2,1)} %get-tuple-element.9, bf16[1024,1,64]{0,2,1:T(8,128)(2,1)S(1)} %get-tuple-element.8, bf16[256,16,64]{2,0,1:T(8,128)(2,1)S(1)} %get-tuple-element.5, ...), kind=kOutput, calls=%fused_computation.72 | convolution fusion | flops 1097335808 | bytes 18366464 | tf_op jit(solution)/shard_map/sub | solution.py:90
  288.0 8.2 %fusion.18 = bf16[128,16,256]{2,0,1:T(8,128)(2,1)} fusion(f32[16,256,1024]{1,2,0:T(8,128)} %get-tuple-element.13, f32[16,256]{1,0:T(8,128)S(1)} %get-tuple-element.12, f32[1024,256]{0,1:T(8,128)} %all-reduce.2.cloned.1.call-done, f32[1024]{0:T(1024)S(1)} %bitcast.55), kind=kOutput, calls=%fused_computation.28 | convolution fusion | flops 1082916864 | bytes 18370560 | tf_op jit(solution)/shard_map/hts,sd->thd/dot_general | solution.py:92
  296.6 81.0 %all-gather.6.cloned.1.call-done = bf16[1024,2048]{0,1:T(8,128)(2,1)} async-done(((bf16[256,2048]{0,1:T(8,128)(2,1)}), bf16[1024,2048]{0,1:T(8,128)(2,1)}) %all-gather.6.cloned.1.call-update) | async-done | bytes 4194320 | tf_op jit(solution)/shard_map/all_gather | solution.py:94
  377.6 23.7 %fusion.45 = f32[1024,4096]{1,0:T(8,128)} fusion(bf16[1024,2048]{0,1:T(8,128)(2,1)} %all-gather.6.cloned.1.call-done, bf16[2048,4096]{1,0:T(8,128)(2,1)} %param.13), kind=kOutput, calls=%fused_computation.73 | convolution fusion | flops 17179869184 | bytes 37748736 | tf_op jit(solution)/shard_map/dot_general | solution.py:97
  402.0 113.9 %reduce-scatter.5.cloned.1.call-done = f32[128,4096]{1,0:T(8,128)} async-done(((f32[1024,4096]{1,0:T(8,128)}), f32[128,4096]{1,0:T(8,128)}) %reduce-scatter.5.cloned.1.call-update) | async-done | bytes 2097168 | tf_op jit(solution)/shard_map/reduce_scatter | solution.py:96
  515.9 2.0 fusion.10
  517.9 11.7 %psum.23 = f32[128]{0:T(128)S(1)} all-reduce(f32[128]{0:T(128)S(1)} %get-tuple-element.2), channel_id=1, replica_groups=mesh['wa'=4,'ha'=8] {'wa'}, use_global_device_ids=true, to_apply=%region_10.11 | all-reduce | flops 128 | bytes 1024 | tf_op jit(solution)/shard_map/psum | solution.py:104
  529.6 1.3 fusion.12
  (36 shorter events, 4.1 us)
Async XLA Ops:
  7.2 59.7 %all-gather.4.cloned.1.call-start = ((), (), s32[]{:S(2)}) async-start(), calls=%async_computation.2 | async-start | bytes 9437184 | tf_op jit(solution)/shard_map/all_gather | solution.py:49
  7.9 117.8 %all-reduce.2.cloned.1.call-start = ((), (), s32[]{:S(2)}) async-start(), calls=%async_computation.3 | async-start | bytes 2097152 | tf_op jit(solution)/shard_map/psum | solution.py:55
  73.6 198.4 %reduce-scatter.3.cloned.1.call-start = ((), (), s32[]{:S(2)}) async-start(), calls=%async_computation.4 | async-start | bytes 10485760 | tf_op jit(solution)/shard_map/reduce_scatter | solution.py:68
  97.7 1.2 copy-start
  97.7 22.2 %copy-start.2 = (s32[1024]{0:T(1024)S(1)}, s32[1024]{0:T(1024)}, u32[]{:S(2)}) copy-start(s32[1024]{0:T(1024)} %param.15) | copy-start | bytes 12292
  97.7 279.9 %all-gather.6.cloned.1.call-start = ((), (), s32[]{:S(2)}) async-start(), calls=%async_computation.5 | async-start | bytes 5242880 | tf_op jit(solution)/shard_map/all_gather | solution.py:94
  296.3 219.6 %reduce-scatter.5.cloned.1.call-start = ((), (), s32[]{:S(2)}) async-start(), calls=%async_computation.6 | async-start | bytes 18874368 | tf_op jit(solution)/shard_map/reduce_scatter | solution.py:96
  401.3 0.7 copy-start.3
  517.9 13.0 %copy-start.1 = (bf16[128,4096]{1,0:T(8,128)(2,1)}, bf16[128,4096]{1,0:T(8,128)(2,1)S(1)}, u32[]{:S(2)}) copy-start(bf16[128,4096]{1,0:T(8,128)(2,1)S(1)} %get-tuple-element.3) | copy-start | bytes 3145732
Sparse Core Ops, SparseCore 0:
  9.9 56.9 all-gather.3
  73.7 51.9 all-reduce.1
  128.1 143.8 reduce-scatter.2
  296.4 81.1 all-gather.5
  401.5 114.3 reduce-scatter.4
where the time goes:
time: 538 us; the launch traced here: 537 us
  waiting for transfers between devices  399 us (74%)
  matrix products  74.5 us (14%)
  blocking collectives  32.3 us (6%)
  between operations  13.9 us (3%)
  other arithmetic  12.1 us (2%)
  local copies, waits for them, and re-layouts  5.39 us (1%)
    reduce_scatter x1, waiting for transfers between devices, on_device(): lax.psum_scatter(jnp.dot(block, w_query, preferred_element_type=jnp.float...  143 us
    reduce_scatter x1, waiting for transfers between devices, on_device(): lax.psum_scatter(jnp.dot(block, w_out, preferred_element_type=jnp.float32...  114 us
    all_gather x1, waiting for transfers between devices, on_device(): head_all = lax.all_gather(head_out, 'wa', axis=0, tiled=True)  81 us
    all_gather x1, waiting for transfers between devices, on_device(): gathered = lax.all_gather(tokens, 'ha', axis=0, tiled=True)  56.5 us
    dot_general x1, matrix products, on_device(): jnp.dot(block, w_query, preferred_element_type=jnp.float32)  24 us
    dot_general x1, matrix products, on_device(): jnp.dot(block, w_out, preferred_element_type=jnp.float32)  23.7 us
    sub x1, matrix products, on_device(): expo = jnp.where(allowed[None], jnp.exp(scores - peak), 0.0)  11.8 us
    psum x1, blocking collectives, on_device(): own_sq = lax.psum(jnp.sum(token_f * token_f, axis=1), 'wa')  11.7 us
  transfers between devices with their start and end apart: 5, of which 5 were waited for; matrix products, arithmetic and copies ran while one was open for 6% of the time, Pallas kernels for 0%

commit v1 on v0

--- a/solution.py
+++ b/solution.py
@@ -5,6 +5,7 @@
 
 KVH = 8
 HD = 128
+WINDOW = 256
 
 
 EPS = 1e-05
@@ -28,6 +29,36 @@
     )
 
 
+def attend(queries, key_head, value_head, segment_ids, first):
+    q_rows = queries.shape[0]
+    size = min(WINDOW, q_rows)
+    keys_pad = jnp.pad(key_head, ((WINDOW, 0), (0, 0)))
+    values_pad = jnp.pad(value_head, ((WINDOW, 0), (0, 0)))
+    segment_pad = jnp.pad(segment_ids, (WINDOW, 0), constant_values=-1)
+    outs = []
+    for at in range(0, q_rows, size):
+        start = first + at
+        query = queries[at : at + size]
+        key = lax.dynamic_slice_in_dim(keys_pad, start, size + WINDOW, 0)
+        value = lax.dynamic_slice_in_dim(values_pad, start, size + WINDOW, 0)
+        k_segment = lax.dynamic_slice_in_dim(segment_pad, start, size + WINDOW, 0)
+        q_segment = lax.dynamic_slice_in_dim(segment_ids, start, size, 0)
+        k_at = jnp.arange(size + WINDOW, dtype=jnp.int32) - WINDOW
+        q_at = jnp.arange(size, dtype=jnp.int32)
+        allowed = (q_segment[:, None] == k_segment[None, :]) & (k_at[None, :] <= q_at[:, None])
+        allowed = allowed & (k_at + start >= 0)[None, :]
+        scores = jnp.einsum(
+            "thd,sd->hts", query, key, preferred_element_type=jnp.float32
+        ) * HD ** (-0.5)
+        scores = jnp.where(allowed[None], scores, -1e30)
+        peak = jnp.max(scores, axis=-1, keepdims=True)
+        expo = jnp.where(allowed[None], jnp.exp(scores - peak), 0.0)
+        weights = (expo / jnp.sum(expo, axis=-1, keepdims=True)).astype(jnp.bfloat16)
+        out = jnp.einsum("hts,sd->thd", weights, value, preferred_element_type=jnp.float32)
+        outs.append(out.astype(jnp.bfloat16))
+    return jnp.concatenate(outs, axis=0)
+
+
 def on_device(tokens, gain_attn, w_query, w_key, w_value, w_out, gain_ffn, segment_ids):
     rows_dev, width_dev = tokens.shape
     n_wa = lax.axis_size("wa")
@@ -47,19 +78,21 @@
         axis=1,
     )
     gathered = lax.all_gather(tokens, "ha", axis=0, tiled=True)
-    own_sq = lax.psum(jnp.sum(token_f * token_f, axis=1), "wa")
-    own_scale = lax.rsqrt(own_sq / width + EPS)
-    row_scale = lax.all_gather(own_scale, "ha", axis=0, tiled=True)
-    scaled = (gathered.astype(jnp.float32) * gain_one).astype(jnp.bfloat16)
+    gathered_f = gathered.astype(jnp.float32)
+    row_sq = jnp.sum(gathered_f * gathered_f, axis=1)
+    scaled = (gathered_f * gain_one).astype(jnp.bfloat16)
     kv_part = jnp.dot(scaled, kv_weights, preferred_element_type=jnp.float32)
-    kv_sum = lax.psum(kv_part, "wa")
+    kv_sum = lax.psum(
+        jnp.concatenate([kv_part, jnp.broadcast_to(row_sq[:, None], (total, HD))], axis=1), "wa"
+    )
+    row_scale = lax.rsqrt(kv_sum[:, 2 * HD] / width + EPS)
     index_all = jnp.arange(total, dtype=jnp.int32)
     fresh = jnp.concatenate([jnp.ones((1,), dtype=bool), segment_ids[1:] != segment_ids[:-1]])
     start_all = lax.cummax(jnp.where(fresh, index_all, jnp.zeros_like(index_all)), axis=0)
     cosine, sine = rope_tables((index_all - start_all).astype(jnp.float32))
     key_plain = (kv_sum[:, :HD] * row_scale[:, None]).astype(jnp.bfloat16)
     key_plain = lax.optimization_barrier(key_plain)
-    value_head = (kv_sum[:, HD:] * row_scale[:, None]).astype(jnp.bfloat16)
+    value_head = (kv_sum[:, HD : 2 * HD] * row_scale[:, None]).astype(jnp.bfloat16)
     key_head = rotate(key_plain.astype(jnp.float32).reshape(total, 1, HD), cosine, sine)
     key_head = key_head.reshape(total, HD).astype(jnp.bfloat16)
     q_rows = total // n_wa
@@ -77,29 +110,17 @@
     queries = rotate(
         (query_f * q_scale[:, None]).reshape(q_rows, heads_dev, HD), q_cos, q_sin
     ).astype(jnp.bfloat16)
-    q_segment = lax.dynamic_slice_in_dim(segment_ids, first, q_rows, 0)
-    q_index = first + jnp.arange(q_rows, dtype=jnp.int32)
-    allowed = (q_segment[:, None] == segment_ids[None, :]) & (
-        index_all[None, :] <= q_index[:, None]
-    )
-    scores = jnp.einsum(
-        "thd,sd->hts", queries, key_head, preferred_element_type=jnp.float32
-    ) * HD ** (-0.5)
-    scores = jnp.where(allowed[None], scores, -1e30)
-    peak = jnp.max(scores, axis=-1, keepdims=True)
-    expo = jnp.where(allowed[None], jnp.exp(scores - peak), 0.0)
-    weights = (expo / jnp.sum(expo, axis=-1, keepdims=True)).astype(jnp.bfloat16)
-    head_out = jnp.einsum("hts,sd->thd", weights, value_head, preferred_element_type=jnp.float32)
-    head_out = head_out.astype(jnp.bfloat16).reshape(q_rows, head_cols)
+    head_out = attend(queries, key_head, value_head, segment_ids, first)
+    head_out = head_out.reshape(q_rows, head_cols)
     head_all = lax.all_gather(head_out, "wa", axis=0, tiled=True)
     block = head_all
     attended = lax.psum_scatter(
-        jnp.dot(block, w_out, preferred_element_type=jnp.float32),
+        jnp.dot(block, w_out, preferred_element_type=jnp.float32).astype(jnp.bfloat16),
         "ha",
         scatter_dimension=0,
         tiled=True,
     )
-    residual_out = (token_f + attended).astype(jnp.bfloat16)
+    residual_out = (token_f + attended.astype(jnp.float32)).astype(jnp.bfloat16)
     residual_f = residual_out.astype(jnp.float32)
     square_two = lax.psum(jnp.sum(residual_f * residual_f, axis=1), "wa")
     scale_two = lax.rsqrt(square_two / width + EPS)

time: 538 us -> 499 us (0.928)
  matrix products: 74.5 us -> 52.8 us
  blocking collectives: 32.3 us -> 11.7 us
  other arithmetic: 12.1 us -> 22.1 us
  waiting for transfers between devices: 399 us -> 393 us
    reduce_scatter x1, waiting for transfers between devices: 114 us -> 69.2 us  [on_device(): lax.psum_scatter(jnp.dot(block, w_out, preferred_element_type=jnp.float32...]
    psum x1, waiting for transfers between devices: 3.33 us -> 42.5 us  [on_device(): lax.psum(jnp.concatenate([kv_part, jnp.broadcast_to(row_sq[:, None], (tot...]
    sub x1 -> x0, matrix products: 11.8 us -> none  [on_device(): expo = jnp.where(allowed[None], jnp.exp(scores - peak), 0.0)]
    psum x1 -> x0, blocking collectives: 11.7 us -> none  [on_device(): own_sq = lax.psum(jnp.sum(token_f * token_f, axis=1), 'wa')]
    all_gather x1 -> x0, blocking collectives: 8.88 us -> none  [on_device(): row_scale = lax.all_gather(own_scale, 'ha', axis=0, tiled=True)]
where the time goes in v1:
time: 499 us
  waiting for transfers between devices  393 us (79%)
  matrix products  52.8 us (11%)
  other arithmetic  22.1 us (4%)
  between operations  13.9 us (3%)
  blocking collectives  11.7 us (2%)
  local copies, waits for them, and re-layouts  5.19 us (1%)
    reduce_scatter x1, waiting for transfers between devices, on_device(): lax.psum_scatter(jnp.dot(block, w_query, preferred_element_type=jnp.float...  143 us
    all_gather x1, waiting for transfers between devices, on_device(): head_all = lax.all_gather(head_out, 'wa', axis=0, tiled=True)  81 us
    reduce_scatter x1, waiting for transfers between devices, on_device(): lax.psum_scatter(jnp.dot(block, w_out, preferred_element_type=jnp.float32...  69.2 us
    all_gather x1, waiting for transfers between devices, on_device(): gathered = lax.all_gather(tokens, 'ha', axis=0, tiled=True)  56.5 us
    psum x1, waiting for transfers between devices, on_device(): lax.psum(jnp.concatenate([kv_part, jnp.broadcast_to(row_sq[:, None], (tot...  42.5 us
    dot_general x1, matrix products, on_device(): jnp.dot(block, w_query, preferred_element_type=jnp.float32)  24.1 us
    dot_general x1, matrix products, on_device(): jnp.dot(block, w_out, preferred_element_type=jnp.float32)  23.2 us
    psum x1, blocking collectives, on_device(): square_two = lax.psum(jnp.sum(residual_f * residual_f, axis=1), 'wa')  11.7 us
  transfers between devices with their start and end apart: 5, of which 5 were waited for; matrix products, arithmetic and copies ran while one was open for 6% of the time, Pallas kernels for 0%

profile of v1, /device:TPU:0, one launch (start us, length us, event | category | flops | bytes accessed | tf_op | source)
XLA Modules:
  0.0 499.1 jit_solution(17607958058642940988)
XLA Ops:
  7.2 0.7 all-gather.3.cloned.1.call-update
  7.9 0.7 convert_element_type.63
  8.7 1.7 constant_dynamic-slice_fusion.1
  10.3 56.5 %all-gather.3.cloned.1.call-done = bf16[1024,4096]{1,0:T(8,128)(2,1)} async-done(((bf16[128,4096]{1,0:T(8,128)(2,1)}), bf16[1024,4096]{1,0:T(8,128)(2,1)}) %all-gather.3.cloned.1.call-update) | async-done | bytes 8388624 | tf_op jit(solution)/shard_map/all_gather | solution.py:80
  66.9 5.2 %fusion.2 = f32[1024]{0:T(1024)S(1)} fusion(bf16[1024,4096]{1,0:T(8,128)(2,1)} %all-gather.3.cloned.1.call-done), kind=kLoop, calls=%fused_computation.4 | loop fusion | flops 12581888 | bytes 8392704 | tf_op jit(solution)/shard_map/reduce_sum | solution.py:82
  72.6 2.4 fusion.5
  75.1 1.3 pad_maximum_fusion
  76.5 24.1 %fusion.3 = f32[1024,2048]{1,0:T(8,128)} fusion(bf16[4096,2048]{1,0:T(8,128)(2,1)} %param.10, bf16[1024,4096]{1,0:T(8,128)(2,1)} %all-gather.3.cloned.1.call-done, f32[4096]{0:T(1024)S(1)} %convert_element_type.63), kind=kOutput, calls=%fused_computation.9 | convolution fusion | flops 17192452096 | bytes 33570816 | tf_op jit(solution)/shard_map/dot_general | solution.py:102
  103.1 42.5 %all-reduce.5.cloned.1.call-done = f32[1024,384]{0,1:T(8,128)} async-done(((f32[1024,384]{0,1:T(8,128)}), f32[1024,384]{0,1:T(8,128)}) %all-reduce.5.cloned.1.call-update) | async-done | bytes 1572880 | tf_op jit(solution)/shard_map/psum | solution.py:85
  145.6 0.8 fusion.40
  146.3 1.3 fusion.24
  147.7 1.2 fusion.32
  148.9 142.8 %reduce-scatter.3.cloned.1.call-done = f32[256,2048]{1,0:T(8,128)} async-done(((f32[1024,2048]{1,0:T(8,128)}), f32[256,2048]{1,0:T(8,128)}) %reduce-scatter.3.cloned.1.call-update) | async-done | bytes 2097168 | tf_op jit(solution)/shard_map/reduce_scatter | solution.py:101
  291.7 1.8 multiply_bitcast_fusion
  294.6 1.4 subtract_convert_fusion
  296.0 1.3 fusion.19
  297.3 4.3 fusion.51
  301.6 1.7 fusion.18
  303.7 81.0 %all-gather.5.cloned.1.call-done = bf16[1024,2048]{0,1:T(8,128)(2,1)} async-done(((bf16[256,2048]{0,1:T(8,128)(2,1)}), bf16[1024,2048]{0,1:T(8,128)(2,1)}) %all-gather.5.cloned.1.call-update) | async-done | bytes 4194320 | tf_op jit(solution)/shard_map/all_gather | solution.py:115
  384.7 23.2 %convolution_convert_fusion = bf16[1024,4096]{1,0:T(8,128)(2,1)} fusion(bf16[1024,2048]{0,1:T(8,128)(2,1)} %all-gather.5.cloned.1.call-done, bf16[2048,4096]{1,0:T(8,128)(2,1)} %param.13), kind=kOutput, calls=%fused_computation.8 | convolution fusion | flops 17184063488 | bytes 29360128 | tf_op jit(solution)/shard_map/dot_general | solution.py:118
  408.7 69.2 %reduce-scatter.5.cloned.1.call-done = bf16[128,4096]{1,0:T(8,128)(2,1)} async-done(((bf16[1024,4096]{1,0:T(8,128)(2,1)}), bf16[128,4096]{1,0:T(8,128)(2,1)}) %reduce-scatter.5.cloned.1.call-update) | async-done | bytes 1048592 | tf_op jit(solution)/shard_map/reduce_scatter | solution.py:117
  477.8 1.7 fusion.12
  479.5 11.7 %psum.15 = f32[128]{0:T(128)S(1)} all-reduce(f32[128]{0:T(128)S(1)} %get-tuple-element.2), channel_id=1, replica_groups=mesh['wa'=4,'ha'=8] {'wa'}, use_global_device_ids=true, to_apply=%region_9.10 | all-reduce | flops 128 | bytes 1024 | tf_op jit(solution)/shard_map/psum | solution.py:125
  491.2 1.3 fusion.14
  (41 shorter events, 5.4 us)
Async XLA Ops:
  7.2 59.7 %all-gather.3.cloned.1.call-start = ((), (), s32[]{:S(2)}) async-start(), calls=%async_computation.2 | async-start | bytes 9437184 | tf_op jit(solution)/shard_map/all_gather | solution.py:80
  7.9 137.7 %all-reduce.5.cloned.1.call-start = ((), (), s32[]{:S(2)}) async-start(), calls=%async_computation.3 | async-start | bytes 3145728 | tf_op jit(solution)/shard_map/psum | solution.py:85
  66.9 5.8 %copy-start = (bf16[1024,4096]{1,0:T(8,128)(2,1)S(1)}, bf16[1024,4096]{1,0:T(8,128)(2,1)}, u32[]{:S(2)}) copy-start(bf16[1024,4096]{1,0:T(8,128)(2,1)} %all-gather.3.cloned.1.call-done) | copy-start | bytes 25165828
  76.4 215.3 %reduce-scatter.3.cloned.1.call-start = ((), (), s32[]{:S(2)}) async-start(), calls=%async_computation.4 | async-start | bytes 10485760 | tf_op jit(solution)/shard_map/reduce_scatter | solution.py:101
  100.6 0.7 copy-start.3
  100.6 284.1 %all-gather.5.cloned.1.call-start = ((), (), s32[]{:S(2)}) async-start(), calls=%async_computation.5 | async-start | bytes 5242880 | tf_op jit(solution)/shard_map/all_gather | solution.py:115
  303.4 174.4 %reduce-scatter.5.cloned.1.call-start = ((), (), s32[]{:S(2)}) async-start(), calls=%async_computation.6 | async-start | bytes 9437184 | tf_op jit(solution)/shard_map/reduce_scatter | solution.py:117
  408.0 0.7 copy-start.4
  408.0 69.9 %copy-start.2 = (bf16[128,4096]{1,0:T(8,128)(2,1)S(1)}, bf16[128,4096]{1,0:T(8,128)(2,1)}, u32[]{:S(2)}) copy-start(bf16[128,4096]{1,0:T(8,128)(2,1)} %param.8) | copy-start | bytes 3145732
  479.5 13.0 %copy-start.1 = (bf16[128,4096]{1,0:T(8,128)(2,1)}, bf16[128,4096]{1,0:T(8,128)(2,1)S(1)}, u32[]{:S(2)}) copy-start(bf16[128,4096]{1,0:T(8,128)(2,1)S(1)} %get-tuple-element.3) | copy-start | bytes 3145732
Sparse Core Ops, SparseCore 0:
  9.9 56.9 all-gather.2
  76.6 68.9 all-reduce.4
  147.9 143.7 reduce-scatter.2
  303.5 81.1 all-gather.4
  408.1 69.6 reduce-scatter.4

commit v2 on v1

--- a/solution.py
+++ b/solution.py
@@ -1,6 +1,10 @@
+import functools
+
 import jax
 import jax.numpy as jnp
 from jax import lax
+from jax.experimental import pallas as pl
+from jax.experimental.pallas import tpu as pltpu
 from jax.sharding import PartitionSpec as P
 
 KVH = 8
@@ -29,18 +33,308 @@
     )
 
 
+def greet_peers(n):
+    me = lax.axis_index("wa")
+    barrier = pltpu.get_barrier_semaphore()
+    for d in range(1, n):
+        pl.semaphore_signal(
+            barrier,
+            inc=1,
+            device_id={"wa": lax.rem(me + d, n)},
+            device_id_type=pl.DeviceIdType.MESH,
+        )
+    pl.semaphore_wait(barrier, n - 1)
+
+
+def send_to(src, dst, send_sem, recv_sem, peer):
+    return pltpu.make_async_remote_copy(
+        src_ref=src,
+        dst_ref=dst,
+        send_sem=send_sem,
+        recv_sem=recv_sem,
+        device_id={"wa": peer},
+        device_id_type=pl.DeviceIdType.MESH,
+    )
+
+
+def peer_copies(n, x_ref, land, sems):
+    me = lax.axis_index("wa")
+    return [
+        send_to(x_ref, land.at[d - 1], sems.at[0, d - 1], sems.at[1, d - 1], lax.rem(me + d, n))
+        for d in range(1, n)
+    ]
+
+
+def peer_sum_kernel(n, x_ref, o_ref, land, sems):
+    greet_peers(n)
+    copies = peer_copies(n, x_ref, land, sems)
+    for copy in copies:
+        copy.start()
+    for copy in copies:
+        copy.wait()
+    total = x_ref[...]
+    for d in range(n - 1):
+        total = total + land[d]
+    o_ref[...] = total
+
+
+def peer_sum(x, n):
+    vmem = pl.BlockSpec(memory_space=pltpu.VMEM)
+    return pl.pallas_call(
+        functools.partial(peer_sum_kernel, n),
+        out_shape=jax.ShapeDtypeStruct(x.shape, x.dtype),
+        in_specs=[vmem],
+        out_specs=vmem,
+        scratch_shapes=[
+            pltpu.VMEM((n - 1,) + x.shape, x.dtype),
+            pltpu.SemaphoreType.DMA((2, n - 1)),
+        ],
+        compiler_params=pltpu.CompilerParams(
+            collective_id=2, has_side_effects=True, vmem_limit_bytes=4 << 20
+        ),
+    )(x)
+
+
+def reduce_kernel(
+    n, nc, half, window, q_ref, kv_ref, sq_ref, qo, kvo, sqo,
+    rq, rkv, lq, lkv, lsq, rqs, rks, lqs, lks, sqs,
+):
+    me = lax.axis_index("wa")
+    last = n - 1
+    right = jnp.minimum(me + 1, last)
+    left = jnp.maximum(me - 1, 0)
+    cq = half // nc
+    cw = (half + window) // nc
+    greet_peers(n)
+    small = peer_copies(n, sq_ref, lsq, sqs)
+    for copy in small:
+        copy.start()
+    kvo[pl.ds(0, window), :] = jnp.zeros((window, kvo.shape[1]), kvo.dtype)
+
+    def rows(base, j, size):
+        return pl.ds(pl.multiple_of(base + j * size, 8), size)
+
+    def right_copy(j, first_hop):
+        own, wide = rows(0, j, cq), rows(0, j, cw)
+        if first_hop:
+            src, src_kv = q_ref.at[rows(half, j, cq)], kv_ref.at[rows(half - window, j, cw)]
+        else:
+            src, src_kv = rq.at[own], rkv.at[wide]
+        return (
+            send_to(src, rq.at[own], rqs.at[0, j], rqs.at[1, j], right),
+            send_to(src_kv, rkv.at[wide], rks.at[0, j], rks.at[1, j], right),
+        )
+
+    def left_copy(j, first_hop):
+        own = rows(0, j, cq)
+        src, src_kv = (q_ref, kv_ref) if first_hop else (lq, lkv)
+        return (
+            send_to(src.at[own], lq.at[own], lqs.at[0, j], lqs.at[1, j], left),
+            send_to(src_kv.at[own], lkv.at[own], lks.at[0, j], lks.at[1, j], left),
+        )
+
+    @pl.loop(0, nc + last)
+    def _(s):
+        j = s - me
+        i = s - (last - me)
+        right_on = (j >= 0) & (j < nc)
+        left_on = (i >= 0) & (i < nc)
+
+        @pl.when(right_on & (me > 0))
+        def _():
+            for copy in right_copy(j, False):
+                copy.wait_recv()
+            own, wide = rows(0, j, cq), rows(0, j, cw)
+            rq[own, :] = rq[own, :] + q_ref[rows(half, j, cq), :]
+            rkv[wide, :] = rkv[wide, :] + kv_ref[rows(half - window, j, cw), :]
+
+        @pl.when(left_on & (me < last))
+        def _():
+            for copy in left_copy(i, False):
+                copy.wait_recv()
+            own = rows(0, i, cq)
+            lq[own, :] = lq[own, :] + q_ref[own, :]
+            lkv[own, :] = lkv[own, :] + kv_ref[own, :]
+
+        @pl.when(right_on & (me == 0))
+        def _():
+            for copy in right_copy(j, True):
+                copy.start()
+
+        @pl.when(left_on & (me == last))
+        def _():
+            for copy in left_copy(i, True):
+                copy.start()
+
+        @pl.when(right_on & (me > 0) & (me < last))
+        def _():
+            for copy in right_copy(j, False):
+                copy.start()
+
+        @pl.when(left_on & (me > 0) & (me < last))
+        def _():
+            for copy in left_copy(i, False):
+                copy.start()
+
+        @pl.when(right_on & (me == last))
+        def _():
+            own, wide = rows(0, j, cq), rows(0, j, cw)
+            qo[own, :] = rq[own, :]
+            kvo[wide, :] = rkv[wide, :]
+
+        @pl.when(left_on & (me < last))
+        def _():
+            own = rows(0, i, cq)
+            qo[own, :] = lq[own, :]
+            kvo[rows(window, i, cq), :] = lkv[own, :]
+
+    @pl.loop(0, nc)
+    def _(j):
+        @pl.when(me < last)
+        def _():
+            for copy in right_copy(j, False):
+                copy.wait_send()
+
+        @pl.when(me > 0)
+        def _():
+            for copy in left_copy(j, False):
+                copy.wait_send()
+
+    for copy in small:
+        copy.wait()
+    total = sq_ref[...]
+    for d in range(n - 1):
+        total = total + lsq[d]
+    sqo[...] = total
+
+
+def reduce_to_ends(q_part, kv_part, row_sq, n, window):
+    rows, cols = q_part.shape
+    kv_cols = kv_part.shape[1]
+    half = rows // 2
+    nc = half // 16
+    vmem = pl.BlockSpec(memory_space=pltpu.VMEM)
+    f32 = jnp.float32
+    pair = pltpu.SemaphoreType.DMA((2, nc))
+    return pl.pallas_call(
+        functools.partial(reduce_kernel, n, nc, half, window),
+        out_shape=(
+            jax.ShapeDtypeStruct((half, cols), f32),
+            jax.ShapeDtypeStruct((half + window, kv_cols), f32),
+            jax.ShapeDtypeStruct(row_sq.shape, f32),
+        ),
+        in_specs=[vmem] * 3,
+        out_specs=(vmem,) * 3,
+        scratch_shapes=[
+            pltpu.VMEM((half, cols), f32),
+            pltpu.VMEM((half + window, kv_cols), f32),
+            pltpu.VMEM((half, cols), f32),
+            pltpu.VMEM((half, kv_cols), f32),
+            pltpu.VMEM((n - 1,) + row_sq.shape, f32),
+            pair,
+            pair,
+            pair,
+            pair,
+            pltpu.SemaphoreType.DMA((2, n - 1)),
+        ],
+        compiler_params=pltpu.CompilerParams(
+            collective_id=0, has_side_effects=True, vmem_limit_bytes=40 << 20
+        ),
+    )(q_part, kv_part, row_sq)
+
+
+def spread_kernel(n, nc, half, x_ref, o_ref, rs, ls):
+    me = lax.axis_index("wa")
+    last = n - 1
+    right = jnp.minimum(me + 1, last)
+    left = jnp.maximum(me - 1, 0)
+    size = half // nc
+    greet_peers(n)
+
+    def rows(base, j):
+        return pl.ds(pl.multiple_of(base + j * size, 16), size)
+
+    def right_copy(j, first_hop):
+        at = rows(0, j)
+        src = x_ref if first_hop else o_ref
+        return send_to(src.at[at], o_ref.at[at], rs.at[0, j], rs.at[1, j], right)
+
+    def left_copy(j, first_hop):
+        at = rows(half, j)
+        src = x_ref.at[rows(0, j)] if first_hop else o_ref.at[at]
+        return send_to(src, o_ref.at[at], ls.at[0, j], ls.at[1, j], left)
+
+    @pl.loop(0, nc + last)
+    def _(s):
+        j = s - me
+        i = s - (last - me)
+        right_on = (j >= 0) & (j < nc)
+        left_on = (i >= 0) & (i < nc)
+
+        @pl.when(right_on & (me == 0))
+        def _():
+            right_copy(j, True).start()
+            o_ref[rows(0, j), :] = x_ref[rows(0, j), :]
+
+        @pl.when(left_on & (me == last))
+        def _():
+            left_copy(i, True).start()
+            o_ref[rows(half, i), :] = x_ref[rows(0, i), :]
+
+        @pl.when(right_on & (me > 0))
+        def _():
+            right_copy(j, False).wait_recv()
+
+        @pl.when(right_on & (me > 0) & (me < last))
+        def _():
+            right_copy(j, False).start()
+
+        @pl.when(left_on & (me < last))
+        def _():
+            left_copy(i, False).wait_recv()
+
+        @pl.when(left_on & (me > 0) & (me < last))
+        def _():
+            left_copy(i, False).start()
+
+    @pl.loop(0, nc)
+    def _(j):
+        @pl.when(me < last)
+        def _():
+            right_copy(j, False).wait_send()
+
+        @pl.when(me > 0)
+        def _():
+            left_copy(j, False).wait_send()
+
+
+def spread_from_ends(x, n):
+    half, cols = x.shape
+    nc = half // 16
+    vmem = pl.BlockSpec(memory_space=pltpu.VMEM)
+    pair = pltpu.SemaphoreType.DMA((2, nc))
+    return pl.pallas_call(
+        functools.partial(spread_kernel, n, nc, half),
+        out_shape=jax.ShapeDtypeStruct((2 * half, cols), x.dtype),
+        in_specs=[vmem],
+        out_specs=vmem,
+        scratch_shapes=[pair, pair],
+        compiler_params=pltpu.CompilerParams(
+            collective_id=1, has_side_effects=True, vmem_limit_bytes=16 << 20
+        ),
+    )(x)
+
+
 def attend(queries, key_head, value_head, segment_ids, first):
     q_rows = queries.shape[0]
     size = min(WINDOW, q_rows)
-    keys_pad = jnp.pad(key_head, ((WINDOW, 0), (0, 0)))
-    values_pad = jnp.pad(value_head, ((WINDOW, 0), (0, 0)))
     segment_pad = jnp.pad(segment_ids, (WINDOW, 0), constant_values=-1)
     outs = []
     for at in range(0, q_rows, size):
         start = first + at
         query = queries[at : at + size]
-        key = lax.dynamic_slice_in_dim(keys_pad, start, size + WINDOW, 0)
-        value = lax.dynamic_slice_in_dim(values_pad, start, size + WINDOW, 0)
+        key = key_head[at : at + size + WINDOW]
+        value = value_head[at : at + size + WINDOW]
         k_segment = lax.dynamic_slice_in_dim(segment_pad, start, size + WINDOW, 0)
         q_segment = lax.dynamic_slice_in_dim(segment_ids, start, size, 0)
         k_at = jnp.arange(size + WINDOW, dtype=jnp.int32) - WINDOW
@@ -82,37 +376,38 @@
     row_sq = jnp.sum(gathered_f * gathered_f, axis=1)
     scaled = (gathered_f * gain_one).astype(jnp.bfloat16)
     kv_part = jnp.dot(scaled, kv_weights, preferred_element_type=jnp.float32)
-    kv_sum = lax.psum(
-        jnp.concatenate([kv_part, jnp.broadcast_to(row_sq[:, None], (total, HD))], axis=1), "wa"
-    )
-    row_scale = lax.rsqrt(kv_sum[:, 2 * HD] / width + EPS)
+    q_part = jnp.dot(scaled, w_query, preferred_element_type=jnp.float32)
+    lanes = min(total, 128)
+    query_f, kv_sum, sq_sum = reduce_to_ends(
+        q_part, kv_part, row_sq.reshape(total // lanes, lanes), n_wa, WINDOW
+    )
+    row_scale = lax.rsqrt(sq_sum.reshape(total) / width + EPS)
+    q_rows = total // 2
+    first = jnp.where(lax.axis_index("wa") == n_wa - 1, q_rows, 0)
+    kv_rows = q_rows + WINDOW
+
+    def around(table):
+        padded = jnp.pad(table, ((WINDOW, 0),) + ((0, 0),) * (table.ndim - 1))
+        return lax.dynamic_slice_in_dim(padded, first, kv_rows, 0)
+
     index_all = jnp.arange(total, dtype=jnp.int32)
     fresh = jnp.concatenate([jnp.ones((1,), dtype=bool), segment_ids[1:] != segment_ids[:-1]])
     start_all = lax.cummax(jnp.where(fresh, index_all, jnp.zeros_like(index_all)), axis=0)
     cosine, sine = rope_tables((index_all - start_all).astype(jnp.float32))
-    key_plain = (kv_sum[:, :HD] * row_scale[:, None]).astype(jnp.bfloat16)
+    scale = around(row_scale)
+    cosine, sine = around(cosine), around(sine)
+    key_plain = (kv_sum[:, :HD] * scale[:, None]).astype(jnp.bfloat16)
     key_plain = lax.optimization_barrier(key_plain)
-    value_head = (kv_sum[:, HD : 2 * HD] * row_scale[:, None]).astype(jnp.bfloat16)
-    key_head = rotate(key_plain.astype(jnp.float32).reshape(total, 1, HD), cosine, sine)
-    key_head = key_head.reshape(total, HD).astype(jnp.bfloat16)
-    q_rows = total // n_wa
-    first = lax.axis_index("wa") * q_rows
-    block = scaled
-    query_f = lax.psum_scatter(
-        jnp.dot(block, w_query, preferred_element_type=jnp.float32),
-        "wa",
-        scatter_dimension=0,
-        tiled=True,
-    )
-    q_scale = lax.dynamic_slice_in_dim(row_scale, first, q_rows, 0)
-    q_cos = lax.dynamic_slice_in_dim(cosine, first, q_rows, 0)
-    q_sin = lax.dynamic_slice_in_dim(sine, first, q_rows, 0)
+    value_head = (kv_sum[:, HD:] * scale[:, None]).astype(jnp.bfloat16)
+    key_head = rotate(key_plain.astype(jnp.float32).reshape(kv_rows, 1, HD), cosine, sine)
+    key_head = key_head.reshape(kv_rows, HD).astype(jnp.bfloat16)
+    q_scale, q_cos, q_sin = scale[WINDOW:], cosine[WINDOW:], sine[WINDOW:]
     queries = rotate(
         (query_f * q_scale[:, None]).reshape(q_rows, heads_dev, HD), q_cos, q_sin
     ).astype(jnp.bfloat16)
     head_out = attend(queries, key_head, value_head, segment_ids, first)
     head_out = head_out.reshape(q_rows, head_cols)
-    head_all = lax.all_gather(head_out, "wa", axis=0, tiled=True)
+    head_all = spread_from_ends(head_out, n_wa)
     block = head_all
     attended = lax.psum_scatter(
         jnp.dot(block, w_out, preferred_element_type=jnp.float32).astype(jnp.bfloat16),
@@ -122,7 +417,9 @@
     )
     residual_out = (token_f + attended.astype(jnp.float32)).astype(jnp.bfloat16)
     residual_f = residual_out.astype(jnp.float32)
-    square_two = lax.psum(jnp.sum(residual_f * residual_f, axis=1), "wa")
+    own_two = jnp.sum(residual_f * residual_f, axis=1)
+    own_two = jnp.pad(own_two, (0, -rows_dev % 128)).reshape(-1, 128)
+    square_two = peer_sum(own_two, n_wa).reshape(-1)[:rows_dev]
     scale_two = lax.rsqrt(square_two / width + EPS)
     ffn_input = (residual_f * scale_two[:, None] * gain_ffn.astype(jnp.float32)).astype(
         jnp.bfloat16

time: 499 us -> 508 us (1.018)
  waiting for transfers between devices: 393 us -> 118 us
  Pallas kernels: 0 us -> 273 us
  other arithmetic: 22.1 us -> 35.3 us
  blocking collectives: 11.7 us -> 0 us
  local copies, waits for them, and re-layouts: 5.19 us -> 14.8 us
    pallas_call x0 -> x3, Pallas kernels: none -> 273 us  [the longest x1 171 us: reduce_to_ends(): pl.pallas_call(functools.partial(reduce_kernel, n, nc, half, window), out...]
    reduce_scatter x1 -> x0, waiting for transfers between devices: 143 us -> none  [on_device(): lax.psum_scatter(jnp.dot(block, w_query, preferred_element_type=jnp.float...]
    all_gather x1 -> x0, waiting for transfers between devices: 81 us -> none  [on_device(): head_all = lax.all_gather(head_out, 'wa', axis=0, tiled=True)]
    psum x1 -> x0, waiting for transfers between devices: 42.5 us -> none  [on_device(): lax.psum(jnp.concatenate([kv_part, jnp.broadcast_to(row_sq[:, None], (tot...]
    sub x1 -> x2, other arithmetic: 4.31 us -> 16.1 us  [attend(): expo = jnp.where(allowed[None], jnp.exp(scores - peak), 0.0)]
    psum x1 -> x0, blocking collectives: 11.7 us -> none  [on_device(): square_two = lax.psum(jnp.sum(residual_f * residual_f, axis=1), 'wa')]
    all_gather x1, waiting for transfers between devices: 56.5 us -> 47.3 us  [on_device(): gathered = lax.all_gather(tokens, 'ha', axis=0, tiled=True)]
  transfers between devices with their start and end apart: 5 -> 2, of which waited for: 5 -> 2; matrix products, arithmetic and copies ran while one was open for 6% -> 2% of each run, Pallas kernels for 0% -> 0%
where the time goes in v2:
time: 508 us; the launch traced here: 507 us
  Pallas kernels  273 us (54%)
  waiting for transfers between devices  118 us (23%)
  matrix products  51.8 us (10%)
  other arithmetic  35.3 us (7%)
  local copies, waits for them, and re-layouts  14.8 us (3%)
  between operations  14.3 us (3%)
    pallas_call x1, Pallas kernels, reduce_to_ends(): pl.pallas_call(functools.partial(reduce_kernel, n, nc, half, window), out...  171 us
    pallas_call x1, Pallas kernels, spread_from_ends(): pl.pallas_call(functools.partial(spread_kernel, n, nc, half), out_shape=j...  96.7 us
    reduce_scatter x1, waiting for transfers between devices, on_device(): lax.psum_scatter(jnp.dot(block, w_out, preferred_element_type=jnp.float32...  70.1 us
    all_gather x1, waiting for transfers between devices, on_device(): gathered = lax.all_gather(tokens, 'ha', axis=0, tiled=True)  47.3 us
    dot_general x1, matrix products, on_device(): jnp.dot(block, w_out, preferred_element_type=jnp.float32)  21.6 us
    dot_general x1, matrix products, on_device(): q_part = jnp.dot(scaled, w_query, preferred_element_type=jnp.float32)  20.3 us
    sub x2, other arithmetic, attend(): expo = jnp.where(allowed[None], jnp.exp(scores - peak), 0.0)  16.1 us
  transfers between devices with their start and end apart: 2, of which 2 were waited for; matrix products, arithmetic and copies ran while one was open for 2% of the time, Pallas kernels for 0%

profile of v2, /device:TPU:0, one launch (start us, length us, event | category | flops | bytes accessed | tf_op | source)
XLA Modules:
  0.0 507.2 jit_solution(14891196093186410088)
XLA Ops:
  11.9 1.9 multiply_cosine_fusion
  15.4 1.2 fusion.35
  16.6 3.0 constant_dynamic-slice_fusion
  19.6 47.3 %all-gather.2.cloned.1.call-done = bf16[1024,4096]{1,0:T(8,128)(2,1)} async-done(((bf16[128,4096]{1,0:T(8,128)(2,1)}), bf16[1024,4096]{1,0:T(8,128)(2,1)}) %all-gather.2.cloned.1.call-update) | async-done | bytes 8388624 | tf_op jit(solution)/shard_map/all_gather | solution.py:374
  66.9 5.2 %fusion.3 = f32[1024]{0:T(1024)S(1)} fusion(bf16[1024,4096]{1,0:T(8,128)(2,1)} %all-gather.2.cloned.1.call-done), kind=kLoop, calls=%fused_computation.5 | loop fusion | flops 12581888 | bytes 8392704 | tf_op jit(solution)/shard_map/reduce_sum | solution.py:376
  72.6 20.3 %fusion.6.q_ref = f32[1024,2048]{1,0:T(8,128)S(1)} fusion(bf16[4096,2048]{1,0:T(8,128)(2,1)} %param.10, bf16[1024,4096]{1,0:T(8,128)(2,1)S(1)} %copy-done, f32[4096]{0:T(1024)S(1)} %convert_element_type.72), kind=kOutput, calls=%fused_computation.14 | convolution fusion | flops 17192452096 | bytes 33570816 | tf_op jit(solution)/shard_map/dot_general | solution.py:379
  93.0 2.3 fusion.4.kv_ref
  95.3 170.6 %shard_map.95 = (f32[512,2048]{1,0:T(8,128)S(1)}, f32[768,256]{1,0:T(8,128)S(1)}, f32[8,128]{1,0:T(8,128)S(1)}) custom-call(f32[1024,2048]{1,0:T(8,128)S(1)} %fusion.6.q_ref, f32[1024,256]{1,0:T(8,128)S(1)} %fusion.4.kv_ref, f32[8,128]{1,0:T(8,128)S(1)} %bitcast.76), custom_call_target="tpu_custom_call" | custom-call | tf_op jit(solution)/shard_map/pallas_call | solution.py:219
  266.4 0.9 copy.33
  267.4 1.3 fusion.53
  269.2 2.7 subtract_convert_fusion
  272.0 4.6 fusion.29
  276.5 1.3 fusion.31
  277.9 9.9 %fusion.56 = (f32[16,256]{1,0:T(8,128)S(1)}, f32[16,256,512]{1,2,0:T(8,128)S(1)}) fusion(f32[512,256,16]{1,0,2:T(8,128)} %fusion.29, pred[256,512]{0,1:T(8,128)(4,1)S(1)} %copy-done.9), kind=kOutput, calls=%fused_computation.103 | output fusion | flops 14680575 | bytes 16924672 | tf_op jit(solution)/shard_map/sub | solution.py:349
  287.8 6.2 %fusion.55 = (f32[16,256]{1,0:T(8,128)S(1)}, f32[16,256,512]{1,2,0:T(8,128)}) fusion(f32[512,256,16]{1,0,2:T(8,128)S(1)} %fusion.31, pred[256,512]{0,1:T(8,128)(4,1)S(1)} %copy-done.8), kind=kOutput, calls=%fused_computation.102 | output fusion | flops 14680575 | bytes 16924672 | tf_op jit(solution)/shard_map/sub | solution.py:349
  294.8 2.6 copy-done.11
  298.2 1.5 pad_maximum_fusion
  299.7 2.9 copy.30.x_ref
  302.6 96.7 %shard_map.96 = bf16[1024,2048]{1,0:T(8,128)(2,1)S(1)} custom-call(bf16[512,2048]{1,0:T(8,128)(2,1)S(1)} %copy.30.x_ref), custom_call_target="tpu_custom_call" | custom-call | tf_op jit(solution)/shard_map/pallas_call | solution.py:316
  399.3 21.6 %convolution_convert_fusion = bf16[1024,4096]{1,0:T(8,128)(2,1)} fusion(bf16[1024,2048]{1,0:T(8,128)(2,1)S(1)} %shard_map.96, bf16[2048,4096]{1,0:T(8,128)(2,1)} %param.13), kind=kOutput, calls=%fused_computation.12 | convolution fusion | flops 17184063488 | bytes 29360128 | tf_op jit(solution)/shard_map/dot_general | solution.py:413
  421.7 70.1 %reduce-scatter.2.cloned.1.call-done = bf16[128,4096]{1,0:T(8,128)(2,1)} async-done(((bf16[1024,4096]{1,0:T(8,128)(2,1)}), bf16[128,4096]{1,0:T(8,128)(2,1)}) %reduce-scatter.2.cloned.1.call-update) | async-done | bytes 1048592 | tf_op jit(solution)/shard_map/reduce_scatter | solution.py:412
  491.8 1.7 fusion.18
  493.5 5.5 %shard_map.97 = f32[1,128]{1,0:T(1,128)S(1)} custom-call(f32[1,128]{1,0:T(1,128)S(1)} %bitcast.77), custom_call_target="tpu_custom_call" | custom-call | tf_op jit(solution)/shard_map/pallas_call | solution.py:83
  499.0 1.3 fusion.20
  (51 shorter events, 10.0 us)
Async XLA Ops:
  7.2 59.7 %all-gather.2.cloned.1.call-start = ((), (), s32[]{:S(2)}) async-start(), calls=%async_computation.1 | async-start | bytes 9437184 | tf_op jit(solution)/shard_map/all_gather | solution.py:374
  7.9 483.9 %reduce-scatter.2.cloned.1.call-start = ((), (), s32[]{:S(2)}) async-start(), calls=%async_computation.2 | async-start | bytes 9437184 | tf_op jit(solution)/shard_map/reduce_scatter | solution.py:412
  13.8 0.8 copy-start.1
  66.9 5.8 %copy-start = (bf16[1024,4096]{1,0:T(8,128)(2,1)S(1)}, bf16[1024,4096]{1,0:T(8,128)(2,1)}, u32[]{:S(2)}) copy-start(bf16[1024,4096]{1,0:T(8,128)(2,1)} %all-gather.2.cloned.1.call-done) | copy-start | bytes 25165828
  72.6 20.3 %copy-start.5 = (bf16[4096,128]{1,0:T(8,128)(2,1)S(1)}, bf16[4096,128]{1,0:T(8,128)(2,1)}, u32[]{:S(2)}) copy-start(bf16[4096,128]{1,0:T(8,128)(2,1)} %get-tuple-element.32) | copy-start | bytes 3145732
  72.6 20.4 %copy-start.6 = (bf16[4096,128]{1,0:T(8,128)(2,1)S(1)}, bf16[4096,128]{1,0:T(8,128)(2,1)}, u32[]{:S(2)}) copy-start(bf16[4096,128]{1,0:T(8,128)(2,1)} %get-tuple-element.33) | copy-start | bytes 3145732
  267.4 1.6 copy-start.2
  267.4 1.8 copy-start.7
  276.5 1.4 copy-start.9
  277.9 9.9 %copy-start.8 = (pred[256,512]{0,1:T(8,128)(4,1)S(1)}, pred[256,512]{0,1:T(8,128)(4,1)}, u32[]{:S(2)}) copy-start(pred[256,512]{0,1:T(8,128)(4,1)} %get-tuple-element.25) | copy-start | bytes 393220
  294.0 3.4 copy-start.11
  421.0 0.7 copy-start.10
  421.0 70.8 %copy-start.4 = (bf16[128,4096]{1,0:T(8,128)(2,1)S(1)}, bf16[128,4096]{1,0:T(8,128)(2,1)}, u32[]{:S(2)}) copy-start(bf16[128,4096]{1,0:T(8,128)(2,1)} %param.8) | copy-start | bytes 3145732
  493.4 6.9 %copy-start.3 = (bf16[128,4096]{1,0:T(8,128)(2,1)}, bf16[128,4096]{1,0:T(8,128)(2,1)S(1)}, u32[]{:S(2)}) copy-start(bf16[128,4096]{1,0:T(8,128)(2,1)S(1)} %get-tuple-element.9) | copy-start | bytes 3145732
Sparse Core Ops, SparseCore 0:
  9.9 56.9 all-gather.1
  421.1 70.6 reduce-scatter.1

commit v3 on v2

--- a/solution.py
+++ b/solution.py
@@ -31,6 +31,9 @@
     return jnp.concatenate(
         [first * cosine - second * sine, second * cosine + first * sine], axis=-1
     )
+
+
+SKEW = 3
 
 
 def greet_peers(n):
@@ -133,10 +136,10 @@
             send_to(src_kv.at[own], lkv.at[own], lks.at[0, j], lks.at[1, j], left),
         )
 
-    @pl.loop(0, nc + last)
+    @pl.loop(0, nc + SKEW * last)
     def _(s):
-        j = s - me
-        i = s - (last - me)
+        j = s - SKEW * me
+        i = s - SKEW * (last - me)
         right_on = (j >= 0) & (j < nc)
         left_on = (i >= 0) & (i < nc)
 
@@ -264,10 +267,10 @@
         src = x_ref.at[rows(0, j)] if first_hop else o_ref.at[at]
         return send_to(src, o_ref.at[at], ls.at[0, j], ls.at[1, j], left)
 
-    @pl.loop(0, nc + last)
+    @pl.loop(0, nc + SKEW * last)
     def _(s):
-        j = s - me
-        i = s - (last - me)
+        j = s - SKEW * me
+        i = s - SKEW * (last - me)
         right_on = (j >= 0) & (j < nc)
         left_on = (i >= 0) & (i < nc)
 
@@ -371,12 +374,20 @@
         ],
         axis=1,
     )
-    gathered = lax.all_gather(tokens, "ha", axis=0, tiled=True)
-    gathered_f = gathered.astype(jnp.float32)
-    row_sq = jnp.sum(gathered_f * gathered_f, axis=1)
-    scaled = (gathered_f * gain_one).astype(jnp.bfloat16)
-    kv_part = jnp.dot(scaled, kv_weights, preferred_element_type=jnp.float32)
-    q_part = jnp.dot(scaled, w_query, preferred_element_type=jnp.float32)
+    deep = width_dev // 2
+    q_part = kv_part = row_sq = 0.0
+    for at in range(0, width_dev, deep):
+        part = slice(at, at + deep)
+        gathered = lax.all_gather(tokens[:, part], "ha", axis=0, tiled=True)
+        if at:
+            gathered, q_part = lax.optimization_barrier((gathered, q_part))
+        gathered_f = gathered.astype(jnp.float32)
+        row_sq = row_sq + jnp.sum(gathered_f * gathered_f, axis=1)
+        scaled = (gathered_f * gain_one[part]).astype(jnp.bfloat16)
+        kv_part = kv_part + jnp.dot(
+            scaled, kv_weights[part], preferred_element_type=jnp.float32
+        )
+        q_part = q_part + jnp.dot(scaled, w_query[part], preferred_element_type=jnp.float32)
     lanes = min(total, 128)
     query_f, kv_sum, sq_sum = reduce_to_ends(
         q_part, kv_part, row_sq.reshape(total // lanes, lanes), n_wa, WINDOW
@@ -408,12 +419,20 @@
     head_out = attend(queries, key_head, value_head, segment_ids, first)
     head_out = head_out.reshape(q_rows, head_cols)
     head_all = spread_from_ends(head_out, n_wa)
-    block = head_all
-    attended = lax.psum_scatter(
-        jnp.dot(block, w_out, preferred_element_type=jnp.float32).astype(jnp.bfloat16),
-        "ha",
-        scatter_dimension=0,
-        tiled=True,
+    col = width_dev // 2
+    attended = jnp.concatenate(
+        [
+            lax.psum_scatter(
+                jnp.dot(
+                    head_all, w_out[:, at : at + col], preferred_element_type=jnp.float32
+                ).astype(jnp.bfloat16),
+                "ha",
+                scatter_dimension=0,
+                tiled=True,
+            )
+            for at in range(0, width_dev, col)
+        ],
+        axis=1,
     )
     residual_out = (token_f + attended.astype(jnp.float32)).astype(jnp.bfloat16)
     residual_f = residual_out.astype(jnp.float32)

time: 508 us -> 462 us (0.909)
  Pallas kernels: 273 us -> 191 us
  waiting for transfers between devices: 118 us -> 145 us
  matrix products: 51.8 us -> 63.7 us
  other arithmetic: 35.3 us -> 27.9 us
    pallas_call x1, Pallas kernels: 171 us -> 129 us  [reduce_to_ends(): pl.pallas_call(functools.partial(reduce_kernel, n, nc, half, window), out...]
    pallas_call x1, Pallas kernels: 96.7 us -> 55.7 us  [spread_from_ends(): pl.pallas_call(functools.partial(spread_kernel, n, nc, half), out_shape=j...]
    reduce_scatter x1 -> x2, waiting for transfers between devices: 70.1 us -> 89.4 us  [on_device(): lax.psum_scatter(jnp.dot(head_all, w_out[:, at:at + col], preferred_eleme...]
    dot_general x3 -> x6, matrix products: 44.3 us -> 59.4 us  [the longest x2 28.1 us: on_device(): jnp.dot(scaled, w_query[part], preferred_element_type=jnp.float32)]
    all_gather x1 -> x2, waiting for transfers between devices: 47.3 us -> 55.2 us  [on_device(): gathered = lax.all_gather(tokens[:, part], 'ha', axis=0, tiled=True)]
  transfers between devices with their start and end apart: 2 -> 4, of which waited for: 2 -> 4; matrix products, arithmetic and copies ran while one was open for 2% -> 8% of each run, Pallas kernels for 0% -> 0%
where the time goes in v3:
time: 462 us; the launch traced here: 459 us
  Pallas kernels  191 us (41%)
  waiting for transfers between devices  145 us (31%)
  matrix products  63.7 us (14%)
  other arithmetic  27.9 us (6%)
  local copies, waits for them, and re-layouts  17.4 us (4%)
  between operations  14.5 us (3%)
    pallas_call x1, Pallas kernels, reduce_to_ends(): pl.pallas_call(functools.partial(reduce_kernel, n, nc, half, window), out...  129 us
    reduce_scatter x2, waiting for transfers between devices, on_device(): lax.psum_scatter(jnp.dot(head_all, w_out[:, at:at + col], preferred_eleme...  89.4 us
    pallas_call x1, Pallas kernels, spread_from_ends(): pl.pallas_call(functools.partial(spread_kernel, n, nc, half), out_shape=j...  55.7 us
    all_gather x2, waiting for transfers between devices, on_device(): gathered = lax.all_gather(tokens[:, part], 'ha', axis=0, tiled=True)  55.2 us
    dot_general x2, matrix products, on_device(): jnp.dot(scaled, w_query[part], preferred_element_type=jnp.float32)  28.1 us
    dot_general x2, matrix products, on_device(): jnp.dot(head_all, w_out[:, at:at + col], preferred_element_type=jnp.float32)  26.5 us
    sub x2, other arithmetic, attend(): expo = jnp.where(allowed[None], jnp.exp(scores - peak), 0.0)  12.8 us
  transfers between devices with their start and end apart: 4, of which 4 were waited for; matrix products, arithmetic and copies ran while one was open for 8% of the time, Pallas kernels for 0%

profile of v3, /device:TPU:0, one launch (start us, length us, event | category | flops | bytes accessed | tf_op | source)
XLA Modules:
  0.0 459.5 jit_solution(4659759179747974728)
XLA Ops:
  7.2 2.3 fusion.79
  13.5 1.9 multiply_cosine_fusion
  17.6 1.7 constant_dynamic-slice_fusion
  19.3 30.5 %all-gather.5.cloned.1.call-done = bf16[1024,2048]{1,0:T(8,128)(2,1)} async-done(((bf16[128,2048]{1,0:T(8,128)(2,1)}), bf16[1024,2048]{1,0:T(8,128)(2,1)}) %all-gather.5.cloned.1.call-update) | async-done | bytes 4194320 | tf_op jit(solution)/shard_map/all_gather | solution.py:381
  49.8 14.4 %fusion.12 = f32[1024,2048]{1,0:T(8,128)} fusion(bf16[4096,2048]{1,0:T(8,128)(2,1)} %param.10, bf16[1024,2048]{1,0:T(8,128)(2,1)} %all-gather.5.cloned.1.call-done, f32[2048]{0:T(1024)S(1)} %get-tuple-element.25), kind=kOutput, calls=%fused_computation.22 | convolution fusion | flops 8596226048 | bytes 20979712 | tf_op jit(solution)/shard_map/dot_general | solution.py:390
  64.2 24.6 %all-gather.3.cloned.1.call-done = bf16[1024,2048]{1,0:T(8,128)(2,1)} async-done(((bf16[128,2048]{1,0:T(8,128)(2,1)}), bf16[1024,2048]{1,0:T(8,128)(2,1)}) %all-gather.3.cloned.1.call-update) | async-done | bytes 4194320 | tf_op jit(solution)/shard_map/all_gather | solution.py:381
  88.9 13.7 %fusion.16.q_ref = f32[1024,2048]{1,0:T(8,128)S(1)} fusion(f32[1024,2048]{1,0:T(8,128)} %fusion.12, bf16[4096,2048]{1,0:T(8,128)(2,1)} %param.10, bf16[1024,2048]{1,0:T(8,128)(2,1)} %all-gather.3.cloned.1.call-done, f32[2048]{0:T(1024)S(1)} %get-tuple-element.24), kind=kOutput, calls=%fused_computation.26 | convolution fusion | flops 8598323200 | bytes 29368320 | tf_op jit(solution)/shard_map/dot_general | solution.py:390
  102.6 3.6 fusion.33
  107.3 1.7 fusion.3
  110.3 129.3 %shard_map.95 = (f32[512,2048]{1,0:T(8,128)S(1)}, f32[768,256]{1,0:T(8,128)S(1)}, f32[8,128]{1,0:T(8,128)S(1)}) custom-call(f32[1024,2048]{1,0:T(8,128)S(1)} %fusion.16.q_ref, f32[1024,256]{1,0:T(8,128)S(1)} %fusion.46.kv_ref, f32[8,128]{1,0:T(8,128)S(1)} %add_bitcast_fusion.sq_ref), custom_call_target="tpu_custom_call" | custom-call | tf_op jit(solution)/shard_map/pallas_call | solution.py:222
  242.8 2.7 subtract_convert_fusion
  248.2 6.3 %fusion.83 = (f32[16,256]{1,0:T(8,128)S(1)}, f32[16,256,512]{1,2,0:T(8,128)}) fusion(f32[512,256,16]{1,0,2:T(8,128)S(1)} %fusion.50, pred[256,512]{0,1:T(8,128)(4,1)S(1)} %copy-done.6), kind=kOutput, calls=%fused_computation.124 | output fusion | flops 14680575 | bytes 16924672 | tf_op jit(solution)/shard_map/sub | solution.py:352
  254.5 6.5 %fusion.82 = (f32[16,256]{1,0:T(8,128)S(1)}, f32[16,256,512]{1,2,0:T(8,128)}) fusion(f32[512,256,16]{1,0,2:T(8,128)S(1)} %fusion.54, pred[256,512]{0,1:T(8,128)(4,1)S(1)} %get-tuple-element.33), kind=kOutput, calls=%fused_computation.123 | output fusion | flops 14680575 | bytes 16924672 | tf_op jit(solution)/shard_map/sub | solution.py:352
  261.8 2.6 copy-done.10
  265.2 1.5 pad_maximum_fusion
  266.7 2.9 copy.30.x_ref
  269.6 55.7 %shard_map.96 = bf16[1024,2048]{1,0:T(8,128)(2,1)S(1)} custom-call(bf16[512,2048]{1,0:T(8,128)(2,1)S(1)} %copy.30.x_ref), custom_call_target="tpu_custom_call" | custom-call | tf_op jit(solution)/shard_map/pallas_call | solution.py:319
  325.4 2.0 copy-done
  327.3 12.6 %fusion.27 = bf16[1024,2048]{1,0:T(8,128)(2,1)} fusion(bf16[1024,2048]{1,0:T(8,128)(2,1)S(1)} %shard_map.96, bf16[2048,4096]{1,0:T(8,128)(2,1)} %param.13), kind=kOutput, calls=%fused_computation.38 | convolution fusion | flops 8592031744 | bytes 16777216 | tf_op jit(solution)/shard_map/dot_general | solution.py:426
  340.0 13.9 %fusion.30 = bf16[1024,2048]{1,0:T(8,128)(2,1)} fusion(bf16[1024,2048]{1,0:T(8,128)(2,1)} %copy-done, bf16[2048,4096]{1,0:T(8,128)(2,1)} %param.13), kind=kOutput, calls=%fused_computation.39 | convolution fusion | flops 8592031744 | bytes 16777216 | tf_op jit(solution)/shard_map/dot_general | solution.py:426
  354.6 35.0 %reduce-scatter.3.cloned.1.call-done = bf16[128,2048]{1,0:T(8,128)(2,1)} async-done(((bf16[1024,2048]{1,0:T(8,128)(2,1)}), bf16[128,2048]{1,0:T(8,128)(2,1)}) %reduce-scatter.3.cloned.1.call-update) | async-done | bytes 524304 | tf_op jit(solution)/shard_map/reduce_scatter | solution.py:425
  389.6 54.4 %reduce-scatter.5.cloned.1.call-done = bf16[128,2048]{1,0:T(8,128)(2,1)} async-done(((bf16[1024,2048]{1,0:T(8,128)(2,1)}), bf16[128,2048]{1,0:T(8,128)(2,1)}) %reduce-scatter.5.cloned.1.call-update) | async-done | bytes 524304 | tf_op jit(solution)/shard_map/reduce_scatter | solution.py:425
  444.0 1.7 fusion.39
  445.7 5.5 %shard_map.97 = f32[1,128]{1,0:T(1,128)S(1)} custom-call(f32[1,128]{1,0:T(1,128)S(1)} %bitcast.76), custom_call_target="tpu_custom_call" | custom-call | tf_op jit(solution)/shard_map/pallas_call | solution.py:86
  (60 shorter events, 17.9 us)
Async XLA Ops:
  7.2 9.0 %copy-start.7 = (bf16[4096]{0:T(1024)(128)(2,1)S(1)}, bf16[4096]{0:T(1024)(128)(2,1)}, u32[]{:S(2)}) copy-start(bf16[4096]{0:T(1024)(128)(2,1)} %param.9) | copy-start | bytes 24580
  7.2 42.6 %all-gather.5.cloned.1.call-start = ((), (), s32[]{:S(2)}) async-start(), calls=%async_computation.3 | async-start | bytes 4718592 | tf_op jit(solution)/shard_map/all_gather | solution.py:381
  9.5 79.3 %all-gather.3.cloned.1.call-start = ((), (), s32[]{:S(2)}) async-start(), calls=%async_computation.2 | async-start | bytes 4718592 | tf_op jit(solution)/shard_map/all_gather | solution.py:381
  10.3 379.3 %reduce-scatter.3.cloned.1.call-start = ((), (), s32[]{:S(2)}) async-start(), calls=%async_computation.4 | async-start | bytes 4718592 | tf_op jit(solution)/shard_map/reduce_scatter | solution.py:425
  102.6 3.6 copy-start.1
  102.6 4.7 %copy-start.2 = (bf16[1024,2048]{1,0:T(8,128)(2,1)S(1)}, bf16[1024,2048]{1,0:T(8,128)(2,1)}, u32[]{:S(2)}) copy-start(bf16[1024,2048]{1,0:T(8,128)(2,1)} %all-gather.3.cloned.1.call-done) | copy-start | bytes 12582916
  241.4 1.4 copy-start.5
  246.8 1.4 copy-start.6
  254.5 6.5 %copy-start.9 = (f32[16,256,512]{1,2,0:T(8,128)S(1)}, f32[16,256,512]{1,2,0:T(8,128)}, u32[]{:S(2)}) copy-start(f32[16,256,512]{1,2,0:T(8,128)} %get-tuple-element.37) | copy-start | bytes 25165828
  261.0 3.4 copy-start.10
  325.4 2.0 copy-start
  340.0 104.0 %reduce-scatter.5.cloned.1.call-start = ((), (), s32[]{:S(2)}) async-start(), calls=%async_computation.5 | async-start | bytes 4718592 | tf_op jit(solution)/shard_map/reduce_scatter | solution.py:425
  353.9 0.7 copy-start.8
  353.9 90.1 %copy-start.4 = (bf16[128,4096]{1,0:T(8,128)(2,1)S(1)}, bf16[128,4096]{1,0:T(8,128)(2,1)}, u32[]{:S(2)}) copy-start(bf16[128,4096]{1,0:T(8,128)(2,1)} %param.8) | copy-start | bytes 3145732
  445.7 6.9 %copy-start.3 = (bf16[128,4096]{1,0:T(8,128)(2,1)}, bf16[128,4096]{1,0:T(8,128)(2,1)S(1)}, u32[]{:S(2)}) copy-start(bf16[128,4096]{1,0:T(8,128)(2,1)S(1)} %get-tuple-element.13) | copy-start | bytes 3145732
Sparse Core Ops, SparseCore 0:
  10.4 39.2 all-gather.4
  52.2 36.5 all-gather.2
  340.1 49.4 reduce-scatter.2
  392.8 51.1 reduce-scatter.4

commit v4 on v2

--- a/solution.py
+++ b/solution.py
@@ -31,6 +31,9 @@
     return jnp.concatenate(
         [first * cosine - second * sine, second * cosine + first * sine], axis=-1
     )
+
+
+SKEW = 3
 
 
 def greet_peers(n):
@@ -133,10 +136,10 @@
             send_to(src_kv.at[own], lkv.at[own], lks.at[0, j], lks.at[1, j], left),
         )
 
-    @pl.loop(0, nc + last)
+    @pl.loop(0, nc + SKEW * last)
     def _(s):
-        j = s - me
-        i = s - (last - me)
+        j = s - SKEW * me
+        i = s - SKEW * (last - me)
         right_on = (j >= 0) & (j < nc)
         left_on = (i >= 0) & (i < nc)
 
@@ -264,10 +267,10 @@
         src = x_ref.at[rows(0, j)] if first_hop else o_ref.at[at]
         return send_to(src, o_ref.at[at], ls.at[0, j], ls.at[1, j], left)
 
-    @pl.loop(0, nc + last)
+    @pl.loop(0, nc + SKEW * last)
     def _(s):
-        j = s - me
-        i = s - (last - me)
+        j = s - SKEW * me
+        i = s - SKEW * (last - me)
         right_on = (j >= 0) & (j < nc)
         left_on = (i >= 0) & (i < nc)
 

time: 508 us -> 424 us (0.83)
  Pallas kernels: 273 us -> 190 us
    pallas_call x1, Pallas kernels: 171 us -> 129 us  [reduce_to_ends(): pl.pallas_call(functools.partial(reduce_kernel, n, nc, half, window), out...]
    pallas_call x1, Pallas kernels: 96.7 us -> 55.7 us  [spread_from_ends(): pl.pallas_call(functools.partial(spread_kernel, n, nc, half), out_shape=j...]
  transfers between devices with their start and end apart: 2 -> 2, of which waited for: 2 -> 2; matrix products, arithmetic and copies ran while one was open for 2% -> 3% of each run, Pallas kernels for 0% -> 0%
where the time goes in v4:
time: 424 us
  Pallas kernels  190 us (45%)
  waiting for transfers between devices  117 us (28%)
  matrix products  51.8 us (12%)
  other arithmetic  35.3 us (8%)
  local copies, waits for them, and re-layouts  14.8 us (3%)
  between operations  14.3 us (3%)
    pallas_call x1, Pallas kernels, reduce_to_ends(): pl.pallas_call(functools.partial(reduce_kernel, n, nc, half, window), out...  129 us
    reduce_scatter x1, waiting for transfers between devices, on_device(): lax.psum_scatter(jnp.dot(block, w_out, preferred_element_type=jnp.float32...  69.3 us
    pallas_call x1, Pallas kernels, spread_from_ends(): pl.pallas_call(functools.partial(spread_kernel, n, nc, half), out_shape=j...  55.7 us
    all_gather x1, waiting for transfers between devices, on_device(): gathered = lax.all_gather(tokens, 'ha', axis=0, tiled=True)  47.3 us
    dot_general x1, matrix products, on_device(): jnp.dot(block, w_out, preferred_element_type=jnp.float32)  21.6 us
    dot_general x1, matrix products, on_device(): q_part = jnp.dot(scaled, w_query, preferred_element_type=jnp.float32)  20.3 us
    sub x2, other arithmetic, attend(): expo = jnp.where(allowed[None], jnp.exp(scores - peak), 0.0)  16.1 us
  transfers between devices with their start and end apart: 2, of which 2 were waited for; matrix products, arithmetic and copies ran while one was open for 3% of the time, Pallas kernels for 0%

profile of v4, /device:TPU:0, one launch (start us, length us, event | category | flops | bytes accessed | tf_op | source)
XLA Modules:
  0.0 424.0 jit_solution(18090039194036877210)
XLA Ops:
  11.9 1.9 multiply_cosine_fusion
  15.4 1.2 fusion.35
  16.6 3.0 constant_dynamic-slice_fusion
  19.6 47.3 %all-gather.2.cloned.1.call-done = bf16[1024,4096]{1,0:T(8,128)(2,1)} async-done(((bf16[128,4096]{1,0:T(8,128)(2,1)}), bf16[1024,4096]{1,0:T(8,128)(2,1)}) %all-gather.2.cloned.1.call-update) | async-done | bytes 8388624 | tf_op jit(solution)/shard_map/all_gather | solution.py:377
  66.9 5.2 %fusion.3 = f32[1024]{0:T(1024)S(1)} fusion(bf16[1024,4096]{1,0:T(8,128)(2,1)} %all-gather.2.cloned.1.call-done), kind=kLoop, calls=%fused_computation.5 | loop fusion | flops 12581888 | bytes 8392704 | tf_op jit(solution)/shard_map/reduce_sum | solution.py:379
  72.6 20.3 %fusion.6.q_ref = f32[1024,2048]{1,0:T(8,128)S(1)} fusion(bf16[4096,2048]{1,0:T(8,128)(2,1)} %param.10, bf16[1024,4096]{1,0:T(8,128)(2,1)S(1)} %copy-done, f32[4096]{0:T(1024)S(1)} %convert_element_type.72), kind=kOutput, calls=%fused_computation.14 | convolution fusion | flops 17192452096 | bytes 33570816 | tf_op jit(solution)/shard_map/dot_general | solution.py:382
  93.0 2.3 fusion.4.kv_ref
  95.3 129.3 %shard_map.95 = (f32[512,2048]{1,0:T(8,128)S(1)}, f32[768,256]{1,0:T(8,128)S(1)}, f32[8,128]{1,0:T(8,128)S(1)}) custom-call(f32[1024,2048]{1,0:T(8,128)S(1)} %fusion.6.q_ref, f32[1024,256]{1,0:T(8,128)S(1)} %fusion.4.kv_ref, f32[8,128]{1,0:T(8,128)S(1)} %bitcast.76), custom_call_target="tpu_custom_call" | custom-call | tf_op jit(solution)/shard_map/pallas_call | solution.py:222
  225.1 0.9 copy.33
  226.0 1.3 fusion.53
  227.9 2.7 subtract_convert_fusion
  230.6 4.6 %fusion.29 = f32[512,256,16]{1,0,2:T(8,128)} fusion(bf16[512,16,64]{2,0,1:T(8,128)(2,1)S(1)} %get-tuple-element.10, bf16[512,16,64]{2,0,1:T(8,128)(2,1)S(1)} %get-tuple-element.11, bf16[768,1,64]{2,0,1:T(8,128)(2,1)S(1)} %get-tuple-element.14, bf16[768,1,64]{2,0,1:T(8,128)(2,1)S(1)} %get-tuple-element.15), kind=kOutput, calls=%fused_computation.45 | convolution fusion | flops 539230208 | bytes 10682368 | tf_op jit(solution)/shard_map/thd,sd->hts/dot_general | solution.py:347
  235.2 1.3 fusion.31
  236.5 9.9 %fusion.56 = (f32[16,256]{1,0:T(8,128)S(1)}, f32[16,256,512]{1,2,0:T(8,128)S(1)}) fusion(f32[512,256,16]{1,0,2:T(8,128)} %fusion.29, pred[256,512]{0,1:T(8,128)(4,1)S(1)} %copy-done.9), kind=kOutput, calls=%fused_computation.103 | output fusion | flops 14680575 | bytes 16924672 | tf_op jit(solution)/shard_map/sub | solution.py:352
  246.4 6.2 %fusion.55 = (f32[16,256]{1,0:T(8,128)S(1)}, f32[16,256,512]{1,2,0:T(8,128)}) fusion(f32[512,256,16]{1,0,2:T(8,128)S(1)} %fusion.31, pred[256,512]{0,1:T(8,128)(4,1)S(1)} %copy-done.8), kind=kOutput, calls=%fused_computation.102 | output fusion | flops 14680575 | bytes 16924672 | tf_op jit(solution)/shard_map/sub | solution.py:352
  253.4 2.6 copy-done.11
  256.8 1.5 pad_maximum_fusion
  258.3 2.9 copy.30.x_ref
  261.3 55.7 %shard_map.96 = bf16[1024,2048]{1,0:T(8,128)(2,1)S(1)} custom-call(bf16[512,2048]{1,0:T(8,128)(2,1)S(1)} %copy.30.x_ref), custom_call_target="tpu_custom_call" | custom-call | tf_op jit(solution)/shard_map/pallas_call | solution.py:319
  317.0 21.6 %convolution_convert_fusion = bf16[1024,4096]{1,0:T(8,128)(2,1)} fusion(bf16[1024,2048]{1,0:T(8,128)(2,1)S(1)} %shard_map.96, bf16[2048,4096]{1,0:T(8,128)(2,1)} %param.13), kind=kOutput, calls=%fused_computation.12 | convolution fusion | flops 17184063488 | bytes 29360128 | tf_op jit(solution)/shard_map/dot_general | solution.py:416
  339.3 69.3 %reduce-scatter.2.cloned.1.call-done = bf16[128,4096]{1,0:T(8,128)(2,1)} async-done(((bf16[1024,4096]{1,0:T(8,128)(2,1)}), bf16[128,4096]{1,0:T(8,128)(2,1)}) %reduce-scatter.2.cloned.1.call-update) | async-done | bytes 1048592 | tf_op jit(solution)/shard_map/reduce_scatter | solution.py:415
  408.6 1.7 fusion.18
  410.3 5.5 %shard_map.97 = f32[1,128]{1,0:T(1,128)S(1)} custom-call(f32[1,128]{1,0:T(1,128)S(1)} %bitcast.77), custom_call_target="tpu_custom_call" | custom-call | tf_op jit(solution)/shard_map/pallas_call | solution.py:86
  415.8 1.3 fusion.20
  (51 shorter events, 10.0 us)
Async XLA Ops:
  7.2 59.7 %all-gather.2.cloned.1.call-start = ((), (), s32[]{:S(2)}) async-start(), calls=%async_computation.1 | async-start | bytes 9437184 | tf_op jit(solution)/shard_map/all_gather | solution.py:377
  7.9 400.7 %reduce-scatter.2.cloned.1.call-start = ((), (), s32[]{:S(2)}) async-start(), calls=%async_computation.2 | async-start | bytes 9437184 | tf_op jit(solution)/shard_map/reduce_scatter | solution.py:415
  13.8 0.8 copy-start.1
  66.9 5.8 %copy-start = (bf16[1024,4096]{1,0:T(8,128)(2,1)S(1)}, bf16[1024,4096]{1,0:T(8,128)(2,1)}, u32[]{:S(2)}) copy-start(bf16[1024,4096]{1,0:T(8,128)(2,1)} %all-gather.2.cloned.1.call-done) | copy-start | bytes 25165828
  72.6 20.3 %copy-start.5 = (bf16[4096,128]{1,0:T(8,128)(2,1)S(1)}, bf16[4096,128]{1,0:T(8,128)(2,1)}, u32[]{:S(2)}) copy-start(bf16[4096,128]{1,0:T(8,128)(2,1)} %get-tuple-element.32) | copy-start | bytes 3145732
  72.6 20.4 %copy-start.6 = (bf16[4096,128]{1,0:T(8,128)(2,1)S(1)}, bf16[4096,128]{1,0:T(8,128)(2,1)}, u32[]{:S(2)}) copy-start(bf16[4096,128]{1,0:T(8,128)(2,1)} %get-tuple-element.33) | copy-start | bytes 3145732
  226.0 1.6 copy-start.2
  226.0 1.8 copy-start.7
  235.2 1.4 copy-start.9
  236.5 9.9 %copy-start.8 = (pred[256,512]{0,1:T(8,128)(4,1)S(1)}, pred[256,512]{0,1:T(8,128)(4,1)}, u32[]{:S(2)}) copy-start(pred[256,512]{0,1:T(8,128)(4,1)} %get-tuple-element.25) | copy-start | bytes 393220
  252.6 3.4 copy-start.11
  338.6 0.7 copy-start.10
  338.6 70.0 %copy-start.4 = (bf16[128,4096]{1,0:T(8,128)(2,1)S(1)}, bf16[128,4096]{1,0:T(8,128)(2,1)}, u32[]{:S(2)}) copy-start(bf16[128,4096]{1,0:T(8,128)(2,1)} %param.8) | copy-start | bytes 3145732
  410.3 6.8 %copy-start.3 = (bf16[128,4096]{1,0:T(8,128)(2,1)}, bf16[128,4096]{1,0:T(8,128)(2,1)S(1)}, u32[]{:S(2)}) copy-start(bf16[128,4096]{1,0:T(8,128)(2,1)S(1)} %get-tuple-element.9) | copy-start | bytes 3145732
Sparse Core Ops, SparseCore 0:
  9.9 56.9 all-gather.1
  338.7 69.8 reduce-scatter.1

commit v5 on v4

--- a/solution.py
+++ b/solution.py
@@ -33,7 +33,7 @@
     )
 
 
-SKEW = 3
+SKEW = 6
 
 
 def greet_peers(n):

time: 424 us -> 438 us (1.033)
  Pallas kernels: 190 us -> 204 us
    pallas_call x1, Pallas kernels: 129 us -> 139 us  [reduce_to_ends(): pl.pallas_call(functools.partial(reduce_kernel, n, nc, half, window), out...]
  transfers between devices with their start and end apart: 2 -> 2, of which waited for: 2 -> 2; matrix products, arithmetic and copies ran while one was open for 3% -> 2% of each run, Pallas kernels for 0% -> 0%
where the time goes in v5:
time: 438 us
  Pallas kernels  204 us (47%)
  waiting for transfers between devices  118 us (27%)
  matrix products  51.8 us (12%)
  other arithmetic  35.3 us (8%)
  local copies, waits for them, and re-layouts  14.8 us (3%)
  between operations  14.3 us (3%)
    pallas_call x1, Pallas kernels, reduce_to_ends(): pl.pallas_call(functools.partial(reduce_kernel, n, nc, half, window), out...  139 us
    reduce_scatter x1, waiting for transfers between devices, on_device(): lax.psum_scatter(jnp.dot(block, w_out, preferred_element_type=jnp.float32...  69.5 us
    pallas_call x1, Pallas kernels, spread_from_ends(): pl.pallas_call(functools.partial(spread_kernel, n, nc, half), out_shape=j...  59.5 us
    all_gather x1, waiting for transfers between devices, on_device(): gathered = lax.all_gather(tokens, 'ha', axis=0, tiled=True)  47.3 us
    dot_general x1, matrix products, on_device(): jnp.dot(block, w_out, preferred_element_type=jnp.float32)  21.6 us
    dot_general x1, matrix products, on_device(): q_part = jnp.dot(scaled, w_query, preferred_element_type=jnp.float32)  20.3 us
    sub x2, other arithmetic, attend(): expo = jnp.where(allowed[None], jnp.exp(scores - peak), 0.0)  16.1 us
  transfers between devices with their start and end apart: 2, of which 2 were waited for; matrix products, arithmetic and copies ran while one was open for 2% of the time, Pallas kernels for 0%

profile of v5, /device:TPU:0, one launch (start us, length us, event | category | flops | bytes accessed | tf_op | source)
XLA Modules:
  0.0 437.5 jit_solution(9963568596568588865)
XLA Ops:
  11.9 1.9 multiply_cosine_fusion
  15.4 1.2 fusion.35
  16.6 3.0 constant_dynamic-slice_fusion
  19.6 47.3 %all-gather.2.cloned.1.call-done = bf16[1024,4096]{1,0:T(8,128)(2,1)} async-done(((bf16[128,4096]{1,0:T(8,128)(2,1)}), bf16[1024,4096]{1,0:T(8,128)(2,1)}) %all-gather.2.cloned.1.call-update) | async-done | bytes 8388624 | tf_op jit(solution)/shard_map/all_gather | solution.py:377
  66.9 5.2 %fusion.3 = f32[1024]{0:T(1024)S(1)} fusion(bf16[1024,4096]{1,0:T(8,128)(2,1)} %all-gather.2.cloned.1.call-done), kind=kLoop, calls=%fused_computation.5 | loop fusion | flops 12581888 | bytes 8392704 | tf_op jit(solution)/shard_map/reduce_sum | solution.py:379
  72.6 20.3 %fusion.6.q_ref = f32[1024,2048]{1,0:T(8,128)S(1)} fusion(bf16[4096,2048]{1,0:T(8,128)(2,1)} %param.10, bf16[1024,4096]{1,0:T(8,128)(2,1)S(1)} %copy-done, f32[4096]{0:T(1024)S(1)} %convert_element_type.72), kind=kOutput, calls=%fused_computation.14 | convolution fusion | flops 17192452096 | bytes 33570816 | tf_op jit(solution)/shard_map/dot_general | solution.py:382
  93.0 2.3 fusion.4.kv_ref
  95.3 138.8 %shard_map.95 = (f32[512,2048]{1,0:T(8,128)S(1)}, f32[768,256]{1,0:T(8,128)S(1)}, f32[8,128]{1,0:T(8,128)S(1)}) custom-call(f32[1024,2048]{1,0:T(8,128)S(1)} %fusion.6.q_ref, f32[1024,256]{1,0:T(8,128)S(1)} %fusion.4.kv_ref, f32[8,128]{1,0:T(8,128)S(1)} %bitcast.76), custom_call_target="tpu_custom_call" | custom-call | tf_op jit(solution)/shard_map/pallas_call | solution.py:222
  234.6 0.9 copy.33
  235.5 1.3 fusion.53
  237.3 2.7 subtract_convert_fusion
  240.1 4.6 %fusion.29 = f32[512,256,16]{1,0,2:T(8,128)} fusion(bf16[512,16,64]{2,0,1:T(8,128)(2,1)S(1)} %get-tuple-element.10, bf16[512,16,64]{2,0,1:T(8,128)(2,1)S(1)} %get-tuple-element.11, bf16[768,1,64]{2,0,1:T(8,128)(2,1)S(1)} %get-tuple-element.14, bf16[768,1,64]{2,0,1:T(8,128)(2,1)S(1)} %get-tuple-element.15), kind=kOutput, calls=%fused_computation.45 | convolution fusion | flops 539230208 | bytes 10682368 | tf_op jit(solution)/shard_map/thd,sd->hts/dot_general | solution.py:347
  244.7 1.3 fusion.31
  246.0 9.9 %fusion.56 = (f32[16,256]{1,0:T(8,128)S(1)}, f32[16,256,512]{1,2,0:T(8,128)S(1)}) fusion(f32[512,256,16]{1,0,2:T(8,128)} %fusion.29, pred[256,512]{0,1:T(8,128)(4,1)S(1)} %copy-done.9), kind=kOutput, calls=%fused_computation.103 | output fusion | flops 14680575 | bytes 16924672 | tf_op jit(solution)/shard_map/sub | solution.py:352
  255.9 6.2 %fusion.55 = (f32[16,256]{1,0:T(8,128)S(1)}, f32[16,256,512]{1,2,0:T(8,128)}) fusion(f32[512,256,16]{1,0,2:T(8,128)S(1)} %fusion.31, pred[256,512]{0,1:T(8,128)(4,1)S(1)} %copy-done.8), kind=kOutput, calls=%fused_computation.102 | output fusion | flops 14680575 | bytes 16924672 | tf_op jit(solution)/shard_map/sub | solution.py:352
  262.9 2.6 copy-done.11
  266.3 1.5 pad_maximum_fusion
  267.8 2.9 copy.30.x_ref
  270.7 59.5 %shard_map.96 = bf16[1024,2048]{1,0:T(8,128)(2,1)S(1)} custom-call(bf16[512,2048]{1,0:T(8,128)(2,1)S(1)} %copy.30.x_ref), custom_call_target="tpu_custom_call" | custom-call | tf_op jit(solution)/shard_map/pallas_call | solution.py:319
  330.3 21.6 %convolution_convert_fusion = bf16[1024,4096]{1,0:T(8,128)(2,1)} fusion(bf16[1024,2048]{1,0:T(8,128)(2,1)S(1)} %shard_map.96, bf16[2048,4096]{1,0:T(8,128)(2,1)} %param.13), kind=kOutput, calls=%fused_computation.12 | convolution fusion | flops 17184063488 | bytes 29360128 | tf_op jit(solution)/shard_map/dot_general | solution.py:416
  352.6 69.5 %reduce-scatter.2.cloned.1.call-done = bf16[128,4096]{1,0:T(8,128)(2,1)} async-done(((bf16[1024,4096]{1,0:T(8,128)(2,1)}), bf16[128,4096]{1,0:T(8,128)(2,1)}) %reduce-scatter.2.cloned.1.call-update) | async-done | bytes 1048592 | tf_op jit(solution)/shard_map/reduce_scatter | solution.py:415
  422.1 1.7 fusion.18
  423.8 5.5 %shard_map.97 = f32[1,128]{1,0:T(1,128)S(1)} custom-call(f32[1,128]{1,0:T(1,128)S(1)} %bitcast.77), custom_call_target="tpu_custom_call" | custom-call | tf_op jit(solution)/shard_map/pallas_call | solution.py:86
  429.4 1.3 fusion.20
  (51 shorter events, 10.0 us)
Async XLA Ops:
  7.2 59.7 %all-gather.2.cloned.1.call-start = ((), (), s32[]{:S(2)}) async-start(), calls=%async_computation.1 | async-start | bytes 9437184 | tf_op jit(solution)/shard_map/all_gather | solution.py:377
  7.9 414.2 %reduce-scatter.2.cloned.1.call-start = ((), (), s32[]{:S(2)}) async-start(), calls=%async_computation.2 | async-start | bytes 9437184 | tf_op jit(solution)/shard_map/reduce_scatter | solution.py:415
  13.8 0.8 copy-start.1
  66.9 5.8 %copy-start = (bf16[1024,4096]{1,0:T(8,128)(2,1)S(1)}, bf16[1024,4096]{1,0:T(8,128)(2,1)}, u32[]{:S(2)}) copy-start(bf16[1024,4096]{1,0:T(8,128)(2,1)} %all-gather.2.cloned.1.call-done) | copy-start | bytes 25165828
  72.6 20.3 %copy-start.5 = (bf16[4096,128]{1,0:T(8,128)(2,1)S(1)}, bf16[4096,128]{1,0:T(8,128)(2,1)}, u32[]{:S(2)}) copy-start(bf16[4096,128]{1,0:T(8,128)(2,1)} %get-tuple-element.32) | copy-start | bytes 3145732
  72.6 20.4 %copy-start.6 = (bf16[4096,128]{1,0:T(8,128)(2,1)S(1)}, bf16[4096,128]{1,0:T(8,128)(2,1)}, u32[]{:S(2)}) copy-start(bf16[4096,128]{1,0:T(8,128)(2,1)} %get-tuple-element.33) | copy-start | bytes 3145732
  235.5 1.6 copy-start.2
  235.5 1.8 copy-start.7
  244.6 1.4 copy-start.9
  246.0 9.9 %copy-start.8 = (pred[256,512]{0,1:T(8,128)(4,1)S(1)}, pred[256,512]{0,1:T(8,128)(4,1)}, u32[]{:S(2)}) copy-start(pred[256,512]{0,1:T(8,128)(4,1)} %get-tuple-element.25) | copy-start | bytes 393220
  262.1 3.4 copy-start.11
  351.9 0.7 copy-start.10
  351.9 70.2 %copy-start.4 = (bf16[128,4096]{1,0:T(8,128)(2,1)S(1)}, bf16[128,4096]{1,0:T(8,128)(2,1)}, u32[]{:S(2)}) copy-start(bf16[128,4096]{1,0:T(8,128)(2,1)} %param.8) | copy-start | bytes 3145732
  423.8 6.8 %copy-start.3 = (bf16[128,4096]{1,0:T(8,128)(2,1)}, bf16[128,4096]{1,0:T(8,128)(2,1)S(1)}, u32[]{:S(2)}) copy-start(bf16[128,4096]{1,0:T(8,128)(2,1)S(1)} %get-tuple-element.9) | copy-start | bytes 3145732
Sparse Core Ops, SparseCore 0:
  9.9 56.9 all-gather.1
  352.1 70.0 reduce-scatter.1
